TPU v7x, 128 devices: a whole 4x4x4 slice. The times are simulated.
128 devices in a mesh: gx: 16 (over x, z_hi, core), gy: 8 (over z_lo, y).
Axes of the slice: x: 4, y: 4, z: 4 (z_hi: 2, z_lo: 2; z = z_hi * 2 + z_lo), core: 2. Of those that a mesh axis runs over, the one named last changes fastest.
Arguments:
- volume: bfloat16 [64, 32, 128, 128], P(None, 'gx', 'gy'), may hold values from -6 to 6
- kernel: bfloat16 [4, 4, 4, 32, 64], replicated, may hold values from -0.25 to 0.25
- cotangent: bfloat16 [2, 2, 2, 32, 32, 128, 128], P(None, None, None, None, 'gx', 'gy'), may hold values from -6 to 6
Outputs:
- activation: bfloat16 [2, 2, 2, 32, 32, 128, 128], P(None, None, None, None, 'gx', 'gy')
- input_grad: bfloat16 [64, 32, 128, 128], P(None, 'gx', 'gy')
- weight_grad: float32 [4, 4, 4, 32, 64], replicated
All inputs are finite; a program needn't handle non-finite values.
Results may differ from a plain program's by a relative error of at most 0.0049.
Values may be sent and summed in bfloat16 or wider, within the bound.
A program may use at most 192 MiB of HBM per device.

v0:
```python
import math

import jax
import jax.numpy as jnp
from jax import lax
from jax.sharding import PartitionSpec as P

FORWARD_TAPS = (((1, 0), (3, -1)), ((2, 0), (0, 1)))
PHASE_TAPS = (((1, 0), (3, 1)), ((0, -1), (2, 0)))


def padded_2(block, sides, width):
    for axis, dim in sides:
        count = lax.axis_size(axis)
        forward = [(i, i + 1) for i in range(count - 1)]
        backward = [(target, source) for source, target in forward]
        low = lax.ppermute(
            lax.slice_in_dim(block, block.shape[dim] - width, None, axis=dim), axis, forward
        )
        high = lax.ppermute(lax.slice_in_dim(block, 0, width, axis=dim), axis, backward)
        block = jnp.concatenate([low, block, high], axis=dim)
    return block


def silu_pair(before):
    sigmoid = jax.nn.sigmoid(before)
    return (before * sigmoid, sigmoid * (1.0 + before * (1.0 - sigmoid)))


def phase_product(padded, kernel, phase_x, phase_y, phase_z, span_x, span_y, depth_cells):
    total = None
    for tap_x, shift_x in FORWARD_TAPS[phase_x]:
        for tap_y, shift_y in FORWARD_TAPS[phase_y]:
            for tap_z, shift_z in FORWARD_TAPS[phase_z]:
                piece = lax.slice(
                    padded,
                    (0, 1 + shift_x, 1 + shift_y, 1 + shift_z),
                    (
                        padded.shape[0],
                        1 + shift_x + span_x,
                        1 + shift_y + span_y,
                        1 + shift_z + depth_cells,
                    ),
                )
                term = lax.dot_general(
                    kernel[tap_x, tap_y, tap_z],
                    piece,
                    (((1,), (0,)), ((), ())),
                    preferred_element_type=jnp.float32,
                )
                total = term if total is None else total + term
    return total


def all_phases(padded, kernel, span_x, span_y, depth_cells):
    results = []
    for phase_x in range(2):
        for phase_y in range(2):
            for phase_z in range(2):
                results.append(
                    phase_product(
                        padded, kernel, phase_x, phase_y, phase_z, span_x, span_y, depth_cells
                    )
                )
    chans_out = results[0].shape[0]
    return jnp.stack(results).reshape(2, 2, 2, chans_out, span_x, span_y, depth_cells)


def on_device(volume, kernel, cotangent):
    cells_x = volume.shape[1]
    cells_y = volume.shape[2]
    depth_cells = volume.shape[3]
    rim_cells = padded_2(volume, (("gx", 1), ("gy", 2)), 1)
    padded = jnp.pad(rim_cells, ((0, 0), (0, 0), (0, 0), (1, 1)))
    before = all_phases(padded, kernel, cells_x, cells_y, depth_cells)
    values, slopes = silu_pair(before)
    activation = values.astype(jnp.bfloat16)
    grad_pre = (cotangent.astype(jnp.float32) * slopes).astype(jnp.bfloat16)
    grad_rim = padded_2(grad_pre, (("gx", 4), ("gy", 5)), 1)
    grad_pad = jnp.pad(grad_rim, ((0, 0), (0, 0), (0, 0), (0, 0), (0, 0), (0, 0), (1, 1)))
    chans_out = grad_pad.shape[3]
    back_sum = None
    weight_parts = [None] * 64
    for phase_x in range(2):
        for phase_y in range(2):
            for phase_z in range(2):
                source = grad_pad[phase_x, phase_y, phase_z]
                group_list = []
                group_slots = []
                for tap_x, shift_x in PHASE_TAPS[phase_x]:
                    for tap_y, shift_y in PHASE_TAPS[phase_y]:
                        for tap_z, shift_z in PHASE_TAPS[phase_z]:
                            piece = lax.slice(
                                source,
                                (0, 1 + shift_x, 1 + shift_y, 1 + shift_z),
                                (
                                    chans_out,
                                    1 + shift_x + cells_x,
                                    1 + shift_y + cells_y,
                                    1 + shift_z + depth_cells,
                                ),
                            )
                            product = lax.dot_general(
                                kernel[tap_x, tap_y, tap_z],
                                piece,
                                (((0,), (0,)), ((), ())),
                                preferred_element_type=jnp.float32,
                            )
                            back_sum = product if back_sum is None else back_sum + product
                            group_list.append(
                                lax.dot_general(
                                    piece,
                                    volume,
                                    (((1, 2, 3), (1, 2, 3)), ((), ())),
                                    preferred_element_type=jnp.float32,
                                )
                            )
                            group_slots.append(16 * tap_x + 4 * tap_y + tap_z)
                group_terms = jnp.stack(group_list)
                for position, flat_index in enumerate(group_slots):
                    weight_parts[flat_index] = group_terms[position]
    input_grad = back_sum.astype(jnp.bfloat16)
    stacked_grad = jnp.stack(weight_parts).reshape(4, 4, 4, chans_out, volume.shape[0])
    stacked_grad = lax.psum(stacked_grad, ("gx", "gy"))
    scaling = 1.0 / math.sqrt(
        cells_x * lax.axis_size("gx") * cells_y * lax.axis_size("gy") * depth_cells
    )
    return (activation, input_grad, stacked_grad * scaling)


def solution(mesh):
    placed = (P(None, "gx", "gy", None), P(), P(None, None, None, None, "gx", "gy", None))
    return jax.shard_map(
        on_device,
        mesh=mesh,
        in_specs=placed,
        out_specs=(P(None, None, None, None, "gx", "gy", None), P(None, "gx", "gy", None), P()),
        check_vma=False,
    )
```

profile of v0, /device:TPU:1, one launch (start us, length us, event | category | flops | bytes accessed | tf_op | source)
XLA Modules:
  0.0 342.6 jit_solution(13506336892047364948)
XLA Ops:
  8.6 6.9 %collective-permute-start = (bf16[64,1,16,128]{3,0,2,1:T(8,128)(2,1)S(1)}, bf16[64,1,16,128]{3,0,2,1:T(8,128)(2,1)S(1)}, u32[]{:S(2)}, u32[]{:S(2)}) collective-permute-start(bf16[64,1,16,128]{3,0,2,1:T(8,128)(2,1)S(1)} %get-tuple-element.25), channel_id=1, source_target_pairs={{0,8},{8,16},{16,24},{24,32},{32,40},{40,48},{48,56},{56,64},{64,7... | collective-permute-start | bytes 786440 | tf_op jit(solution)/shard_map/ppermute | solution.py:17
  15.5 1.9 collective-permute-start.1
  20.0 4.7 %collective-permute-done.1 = bf16[64,1,16,128]{3,0,2,1:T(8,128)(2,1)S(1)} collective-permute-done((bf16[64,1,16,128]{3,0,2,1:T(8,128)(2,1)S(1)}, bf16[64,1,16,128]{3,0,2,1:T(8,128)(2,1)S(1)}, u32[]{:S(2)}, u32[]{:S(2)}) %collective-permute-start.1) | collective-permute-done | bytes 262176 | tf_op jit(solution)/shard_map/ppermute | solution.py:20
  24.7 3.2 collective-permute-start.2
  31.0 2.0 collective-permute-done.3
  33.0 1.8 fusion.11
  49.2 2.5 multiply_convert_fusion
  52.1 3.4 collective-permute-start.4
  55.5 1.9 collective-permute-start.5
  57.4 23.8 %collective-permute-done.4 = bf16[2,2,2,32,1,16,128]{6,3,5,4,2,1,0:T(8,128)(2,1)S(1)} collective-permute-done((bf16[2,2,2,32,1,16,128]{6,3,5,4,2,1,0:T(8,128)(2,1)S(1)}, bf16[2,2,2,32,1,16,128]{6,3,5,4,2,1,0:T(8,128)(2,1)S(1)}, u32[]{:S(2)}, u32[]{:S(2)}) %collective-permute-start.4) | collective-permute-done | bytes 1048608 | tf_op jit(solution)/shard_map/ppermute | solution.py:17
  83.9 2.1 copy.84
  86.1 3.7 %collective-permute-done.7 = bf16[2,2,2,32,4,1,128]{6,3,5,4,2,1,0:T(8,128)(2,1)S(1)} collective-permute-done((bf16[2,2,2,32,4,1,128]{6,3,5,4,2,1,0:T(8,128)(2,1)S(1)}, bf16[2,2,2,32,4,1,128]{6,3,5,4,2,1,0:T(8,128)(2,1)S(1)}, u32[]{:S(2)}, u32[]{:S(2)}) %collective-permute-start.7) | collective-permute-done | bytes 262176 | tf_op jit(solution)/shard_map/ppermute | solution.py:20
  89.8 8.8 %select_maximum_fusion = bf16[2,2,2,32,4,18,130]{6,3,5,4,2,1,0:T(8,128)(2,1)S(1)} fusion(bf16[2,2,2,32,4,1,128]{6,3,5,4,2,1,0:T(8,128)(2,1)S(1)} %collective-permute-done.7, bf16[2,2,2,32,4,1,128]{6,3,5,4,2,1,0:T(8,128)(2,1)S(1)} %collective-permute-done.6, bf16[2,2,2,32,1,16,128]{6,3,5,4,2,1,0:T(8,128)(2,1)S(1)} %collective-permute-done.5, ...), kind=kLoop, calls=%fused_computation.3 | loop fusion | flops 43130880 | bytes 9510912 | tf_op jit(solution)/shard_map/concatenate | solution.py:21
  99.8 1.7 convolution_bitcast_fusion.40
  101.6 1.8 convolution_bitcast_fusion.41
  103.4 1.4 convolution_bitcast_fusion.42
  106.1 1.4 convolution_bitcast_fusion.44
  112.8 1.4 convolution_bitcast_fusion.34
  118.2 1.4 convolution_bitcast_fusion.31
  129.1 1.4 convolution_bitcast_fusion.16
  134.5 1.4 convolution_bitcast_fusion.20
  145.6 1.4 convolution_bitcast_fusion.8
  146.9 1.4 convolution_bitcast_fusion.9
  151.0 1.5 convolution_bitcast_fusion.2
  180.1 1.9 convolution_add_fusion.15
  188.2 1.8 fusion.54
  190.5 1.9 fusion.59
  193.9 1.9 fusion.58
  197.2 1.9 fusion.57
  200.4 1.9 fusion.56
  208.4 124.8 %all-reduce.4.cloned.1.call-done = f32[4,4,4,32,64]{4,3,2,1,0:T(8,128)} async-done(((f32[4,4,4,32,64]{4,3,2,1,0:T(8,128)}), f32[4,4,4,32,64]{4,3,2,1,0:T(8,128)}) %all-reduce.4.cloned.1.call-update) | async-done | bytes 524304 | tf_op jit(solution)/shard_map/psum | solution.py:124
  333.2 2.3 broadcast_multiply_fusion
  (301 shorter events, 106.1 us)
Async XLA Ops:
  7.2 10.3 %copy-start = (bf16[64,2,16,128]{3,2,1,0:T(8,128)(2,1)S(1)}, bf16[64,2,16,128]{3,2,1,0:T(8,128)(2,1)}, u32[]{:S(2)}) copy-start(bf16[64,2,16,128]{3,2,1,0:T(8,128)(2,1)} %param.3) | copy-start | bytes 1572868
  7.2 10.3 %copy-start.51 = (bf16[4,4,4,32,64]{4,3,2,1,0:T(8,128)(2,1)S(1)}, bf16[4,4,4,32,64]{4,3,2,1,0:T(8,128)(2,1)}, u32[]{:S(2)}) copy-start(bf16[4,4,4,32,64]{4,3,2,1,0:T(8,128)(2,1)} %param.4) | copy-start | bytes 786436
  7.2 326.0 %all-reduce.4.cloned.1.call-start = ((), (), s32[]{:S(2)}) async-start(), calls=%async_computation | async-start | bytes 2097152 | tf_op jit(solution)/shard_map/psum | solution.py:124
  8.6 11.1 %collective-permute-start = (bf16[64,1,16,128]{3,0,2,1:T(8,128)(2,1)S(1)}, bf16[64,1,16,128]{3,0,2,1:T(8,128)(2,1)S(1)}, u32[]{:S(2)}, u32[]{:S(2)}) collective-permute-start(bf16[64,1,16,128]{3,0,2,1:T(8,128)(2,1)S(1)} %get-tuple-element.25), channel_id=1, source_target_pairs={{0,8},{8,16},{16,24},{24,32},{32,40},{40,48},{48,56},{56,64},{64,7... | collective-permute-start | bytes 786440 | tf_op jit(solution)/shard_map/ppermute | solution.py:17
  15.5 9.2 %collective-permute-start.1 = (bf16[64,1,16,128]{3,0,2,1:T(8,128)(2,1)S(1)}, bf16[64,1,16,128]{3,0,2,1:T(8,128)(2,1)S(1)}, u32[]{:S(2)}, u32[]{:S(2)}) collective-permute-start(bf16[64,1,16,128]{3,0,2,1:T(8,128)(2,1)S(1)} %get-tuple-element.24), channel_id=1, source_target_pairs={{8,0},{16,8},{24,16},{32,24},{40,32},{48,40},{56,48},{64,56},{72,6... | collective-permute-start | bytes 786440 | tf_op jit(solution)/shard_map/ppermute | solution.py:20
  24.7 6.2 %collective-permute-start.2 = (bf16[64,4,1,128]{3,0,2,1:T(8,128)(2,1)S(1)}, bf16[64,4,1,128]{3,0,2,1:T(8,128)(2,1)S(1)}, u32[]{:S(2)}, u32[]{:S(2)}) collective-permute-start(bf16[64,4,1,128]{3,0,2,1:T(8,128)(2,1)S(1)} %get-tuple-element.22), channel_id=1, source_target_pairs={{0,1},{1,2},{2,3},{3,4},{4,5},{5,6},{6,7},{8,9},{9,10},{10,11},{11... | collective-permute-start | bytes 196616 | tf_op jit(solution)/shard_map/ppermute | solution.py:17
  28.0 5.0 %collective-permute-start.3 = (bf16[64,4,1,128]{3,0,2,1:T(8,128)(2,1)S(1)}, bf16[64,4,1,128]{3,0,2,1:T(8,128)(2,1)S(1)}, u32[]{:S(2)}, u32[]{:S(2)}) collective-permute-start(bf16[64,4,1,128]{3,0,2,1:T(8,128)(2,1)S(1)} %get-tuple-element.23), channel_id=1, source_target_pairs={{1,0},{2,1},{3,2},{4,3},{5,4},{6,5},{7,6},{9,8},{10,9},{11,10},{12... | collective-permute-start | bytes 196616 | tf_op jit(solution)/shard_map/ppermute | solution.py:20
  52.1 29.1 %collective-permute-start.4 = (bf16[2,2,2,32,1,16,128]{6,3,5,4,2,1,0:T(8,128)(2,1)S(1)}, bf16[2,2,2,32,1,16,128]{6,3,5,4,2,1,0:T(8,128)(2,1)S(1)}, u32[]{:S(2)}, u32[]{:S(2)}) collective-permute-start(bf16[2,2,2,32,1,16,128]{6,3,5,4,2,1,0:T(8,128)(2,1)S(1)} %get-tuple-element.18), channel_id=1, source_target_pairs={{0,8},{8,16},{16,24},{24,32},{32,40},{40,48},{48,56},{56,64},{64,7... | collective-permute-start | bytes 3145736 | tf_op jit(solution)/shard_map/ppermute | solution.py:17
  55.5 25.8 %collective-permute-start.5 = (bf16[2,2,2,32,1,16,128]{6,3,5,4,2,1,0:T(8,128)(2,1)S(1)}, bf16[2,2,2,32,1,16,128]{6,3,5,4,2,1,0:T(8,128)(2,1)S(1)}, u32[]{:S(2)}, u32[]{:S(2)}) collective-permute-start(bf16[2,2,2,32,1,16,128]{6,3,5,4,2,1,0:T(8,128)(2,1)S(1)} %get-tuple-element.19), channel_id=1, source_target_pairs={{8,0},{16,8},{24,16},{32,24},{40,32},{48,40},{56,48},{64,56},{72,6... | collective-permute-start | bytes 3145736 | tf_op jit(solution)/shard_map/ppermute | solution.py:20
  81.3 4.8 %collective-permute-start.6 = (bf16[2,2,2,32,4,1,128]{6,3,5,4,2,1,0:T(8,128)(2,1)S(1)}, bf16[2,2,2,32,4,1,128]{6,3,5,4,2,1,0:T(8,128)(2,1)S(1)}, u32[]{:S(2)}, u32[]{:S(2)}) collective-permute-start(bf16[2,2,2,32,4,1,128]{6,3,5,4,2,1,0:T(8,128)(2,1)S(1)} %get-tuple-element.14), channel_id=1, source_target_pairs={{0,1},{1,2},{2,3},{3,4},{4,5},{5,6},{6,7},{8,9},{9,10},{10,11},{11... | collective-permute-start | bytes 786440 | tf_op jit(solution)/shard_map/ppermute | solution.py:17
  82.6 7.1 %collective-permute-start.7 = (bf16[2,2,2,32,4,1,128]{6,3,5,4,2,1,0:T(8,128)(2,1)S(1)}, bf16[2,2,2,32,4,1,128]{6,3,5,4,2,1,0:T(8,128)(2,1)S(1)}, u32[]{:S(2)}, u32[]{:S(2)}) collective-permute-start(bf16[2,2,2,32,4,1,128]{6,3,5,4,2,1,0:T(8,128)(2,1)S(1)} %get-tuple-element.15), channel_id=1, source_target_pairs={{1,0},{2,1},{3,2},{4,3},{5,4},{6,5},{7,6},{9,8},{10,9},{11,10},{12... | collective-permute-start | bytes 786440 | tf_op jit(solution)/shard_map/ppermute | solution.py:20
  99.8 73.0 %copy-start.1 = (bf16[32,4,18,130]{3,0,2,1:T(8,128)(2,1)}, bf16[32,4,18,130]{3,0,2,1:T(8,128)(2,1)S(1)}, u32[]{:S(2)}) copy-start(bf16[32,4,18,130]{3,0,2,1:T(8,128)(2,1)S(1)} %get-tuple-element.8) | copy-start | bytes 1797124
  99.8 73.3 %copy-start.2 = (bf16[32,4,18,130]{3,0,2,1:T(8,128)(2,1)}, bf16[32,4,18,130]{3,0,2,1:T(8,128)(2,1)S(1)}, u32[]{:S(2)}) copy-start(bf16[32,4,18,130]{3,0,2,1:T(8,128)(2,1)S(1)} %get-tuple-element.9) | copy-start | bytes 1797124
  99.8 77.2 %copy-start.3 = (bf16[32,4,18,130]{3,0,2,1:T(8,128)(2,1)}, bf16[32,4,18,130]{3,0,2,1:T(8,128)(2,1)S(1)}, u32[]{:S(2)}) copy-start(bf16[32,4,18,130]{3,0,2,1:T(8,128)(2,1)S(1)} %get-tuple-element.10) | copy-start | bytes 1797124
  99.8 77.6 %copy-start.4 = (bf16[32,4,18,130]{3,0,2,1:T(8,128)(2,1)}, bf16[32,4,18,130]{3,0,2,1:T(8,128)(2,1)S(1)}, u32[]{:S(2)}) copy-start(bf16[32,4,18,130]{3,0,2,1:T(8,128)(2,1)S(1)} %get-tuple-element.11) | copy-start | bytes 1797124
  99.8 78.6 %copy-start.5 = (bf16[32,4,18,130]{3,0,2,1:T(8,128)(2,1)}, bf16[32,4,18,130]{3,0,2,1:T(8,128)(2,1)S(1)}, u32[]{:S(2)}) copy-start(bf16[32,4,18,130]{3,0,2,1:T(8,128)(2,1)S(1)} %get-tuple-element.6) | copy-start | bytes 1797124
  99.8 78.9 %copy-start.7 = (bf16[32,4,18,130]{3,0,2,1:T(8,128)(2,1)}, bf16[32,4,18,130]{3,0,2,1:T(8,128)(2,1)S(1)}, u32[]{:S(2)}) copy-start(bf16[32,4,18,130]{3,0,2,1:T(8,128)(2,1)S(1)} %get-tuple-element.12) | copy-start | bytes 1797124
  187.0 3.0 copy-start.49
  187.4 2.6 copy-start.47
  190.5 2.6 copy-start.40
  190.5 3.0 copy-start.41
  190.5 3.3 copy-start.42
  193.8 2.6 copy-start.33
  193.9 2.9 copy-start.34
  193.9 3.2 copy-start.35
  197.1 2.7 copy-start.26
  197.1 3.0 copy-start.27
  197.1 3.3 copy-start.28
  200.4 2.7 copy-start.19
  200.4 3.0 copy-start.20
  200.4 3.3 copy-start.21
  203.7 2.8 copy-start.14
  (30 other events, 59.8 us)
Sparse Core Ops, SparseCore 0:
  180.2 152.9 all-reduce.3
where the time goes:
time: 346 us; the launch traced here: 343 us
  waiting for transfers between devices  159 us (46%)
  matrix products  114 us (33%)
  starting transfers between devices  21.2 us (6%)
  local copies, waits for them, and re-layouts  17.6 us (5%)
  other arithmetic  15.5 us (4%)
  between operations  15.3 us (4%)
    psum x1, waiting for transfers between devices, on_device(): stacked_grad = lax.psum(stacked_grad, ('gx', 'gy'))  125 us
    dot_general x64, matrix products, on_device(): lax.dot_general(kernel[tap_x, tap_y, tap_z], piece, (((0,), (0,)), ((), (...  75.5 us
    ppermute x4, waiting for transfers between devices, padded_2(): lax.ppermute(lax.slice_in_dim(block, block.shape[dim] - width, None, axis...  23.8 us
    dot_general x64, matrix products, on_device(): lax.dot_general(piece, volume, (((1, 2, 3), (1, 2, 3)), ((), ())), prefer...  21.3 us
    dot_general x64, matrix products, phase_product(): lax.dot_general(kernel[tap_x, tap_y, tap_z], piece, (((1,), (0,)), ((), (...  17 us
    unnamed x111, local copies, waits for them, and re-layouts  15.9 us
    ppermute x4, starting transfers between devices, padded_2(): lax.ppermute(lax.slice_in_dim(block, block.shape[dim] - width, None, axis...  14.8 us
    concatenate x3, other arithmetic, padded_2(): block = jnp.concatenate([low, block, high], axis=dim)  10.7 us
  transfers between devices with their start and end apart: 9, of which 5 were waited for; matrix products, arithmetic and copies ran while one was open for 7% of the time, Pallas kernels for 0%

commit v1 on v0

v1 whole, which is shorter than its diff:
```python
import functools
import math

import jax
import jax.numpy as jnp
from jax import lax
from jax.experimental import pallas as pl
from jax.experimental.pallas import tpu as pltpu
from jax.sharding import PartitionSpec as P

BF = jnp.bfloat16
F32 = jnp.float32
MESH = pl.DeviceIdType.MESH
BACK = ((1, -1), (0, 0), (1, 0), (0, 1))
ROWS = 16
WIDE = ROWS * 128
HALO = (ROWS + 2) * 128


def remote(src, dst, send, recv, device):
    return pltpu.make_async_remote_copy(
        src_ref=src, dst_ref=dst, send_sem=send, recv_sem=recv,
        device_id=device, device_id_type=MESH,
    )


def nt_dot(a, b):
    return lax.dot_general(a, b, (((1,), (1,)), ((), ())), preferred_element_type=F32)


def lanes(start, size):
    return pl.ds(pl.multiple_of(start, 128), size)


def step_kernel(
    scaling, vol_ref, ker_ref, cot_ref, act_ref, ig_ref, wg_ref,
    volb, face, turn, vt, cotb, cotf, actf, actb, g_s, ak, bk, w_s,
    w_send, w_recv, w_bf, rs_in, part, z_in, fin,
    igf, igb, igy, rx, ry, rc, igo, wgo,
    l_sem, o_sem, fs, fr, bs, br, ws, wr,
):
    gx, gy = lax.axis_index("gx"), lax.axis_index("gy")
    core = lax.rem(gx, 2)
    x, z_hi = gx // 4, lax.rem(gx // 2, 2)
    z_lo, y = gy // 4, lax.rem(gy, 4)
    z = 2 * z_hi + z_lo
    other = 1 - core
    far_gx = lax.rem(gx + 15 + 2 * core, 16)
    sib_gx = gx + 1 - 2 * core
    low_gy, high_gy = lax.rem(gy + 7, 8), lax.rem(gy + 1, 8)
    first_y, last_y = gy == 0, gy == 7
    no_far = jnp.logical_or(gx == 0, gx == 15)

    def plane_peer(i):
        px, py = lax.rem(x + i // 4, 4), lax.rem(y + i % 4, 4)
        return px * 4 + py, (px * 4 + 2 * z_hi + core, 4 * z_lo + py)

    def z_peer(i):
        pz = lax.rem(z + i, 4)
        return (4 * x + 2 * (pz // 2) + core, 4 * lax.rem(pz, 2) + y)

    neighbours = [
        (far_gx, gy), (sib_gx, gy), (gx, low_gy), (gx, high_gy),
        (far_gx, low_gy), (far_gx, high_gy), (sib_gx, low_gy), (sib_gx, high_gy),
    ]
    peers = neighbours + [plane_peer(i)[1] for i in range(1, 16)] + [z_peer(i) for i in range(1, 4)]

    vol_copy = pltpu.make_async_copy(vol_ref, volb, l_sem.at[4])
    vol_copy.start()
    blocks = [(1, 0), (0, 1), (other, other), (core, core)]
    cot_copies = []
    for k, (p, m) in enumerate(blocks):
        copy = pltpu.make_async_copy(
            cot_ref.at[pl.ds(4 * p, 4), :, m], cotb.at[k], l_sem.at[k]
        )
        copy.start()
        cot_copies.append(copy)

    barrier = pltpu.get_barrier_semaphore()
    for peer in peers:
        pl.semaphore_signal(barrier, inc=1, device_id=peer, device_id_type=MESH)

    for p in range(2):
        for q in range(2):
            pieces = [
                ker_ref[a, b].reshape(128, 64)
                for a in (1 + p, 3 - 3 * p)
                for b in (1 + q, 3 - 3 * q)
            ]
            ak[p, q] = jnp.concatenate(pieces, axis=1)
    for a in range(4):
        bk[a] = ker_ref[a].reshape(512, 64).astype(F32).T.astype(BF)
    g_s[:, :, :, :, 0:256] = jnp.zeros((2, 2, 2, 128, 256), BF)
    g_s[:, :, :, :, 256 + WIDE:] = jnp.zeros((2, 2, 2, 128, 256), BF)

    vol_copy.wait()
    pl.semaphore_wait(barrier, len(peers))

    sends = [
        remote(volb.at[:, core], face.at[0], fs.at[0], fr.at[0], neighbours[0]),
        remote(volb.at[:, other], face.at[1], fs.at[1], fr.at[1], neighbours[1]),
    ]
    for copy in sends:
        copy.start()

    def turn_in(get, slot):
        turn[...] = get().astype(F32).reshape(64 * ROWS, 128)

        def row(n, _):
            vt[slot, :, lanes((n + 1) * 128, 128)] = turn[pl.ds(n, 64, stride=ROWS), :].astype(BF)
            return 0

        lax.fori_loop(0, ROWS, row, 0, unroll=True)

    turn_in(lambda: volb[:, 0], 1)
    turn_in(lambda: volb[:, 1], 2)

    first, last = pl.ds(128, 128), pl.ds(ROWS * 128, 128)
    low, high = pl.ds(0, 128), pl.ds((ROWS + 1) * 128, 128)
    own = pl.ds(1, 2)
    ysends = [
        remote(vt.at[own, :, first], vt.at[own, :, high], fs.at[2], fr.at[2], neighbours[2]),
        remote(vt.at[own, :, last], vt.at[own, :, low], fs.at[3], fr.at[3], neighbours[3]),
    ]
    for k, (m, slot) in enumerate(((core, 3 - 3 * core), (other, 3 * core))):
        base = 4 + 2 * k
        ysends.append(remote(vt.at[1 + m, :, first], vt.at[slot, :, high], fs.at[base], fr.at[base], neighbours[base]))
        ysends.append(remote(vt.at[1 + m, :, last], vt.at[slot, :, low], fs.at[base + 1], fr.at[base + 1], neighbours[base + 1]))
    for copy in ysends:
        copy.start()
    sends += ysends

    lane = lax.broadcasted_iota(jnp.int32, (32, 128), 1)

    def up(u):
        return jnp.where(lane == 0, 0.0, pltpu.roll(u, 1, axis=1))

    def down(u):
        return jnp.where(lane == 127, 0.0, pltpu.roll(u, 127, axis=1))

    def stacked(near, far, q, start, size):
        shift = 2 * q
        return jnp.concatenate(
            [
                vt[near, :, lanes(start + 128, size)],
                vt[near, :, lanes(start + 128 * shift, size)],
                vt[far, :, lanes(start + 128, size)],
                vt[far, :, lanes(start + 128 * shift, size)],
            ],
            axis=0,
        )

    def block(k):
        p, m = blocks[k]
        near, far = m + 1, m + 2 * p
        cot_copies[k].wait()
        cotf[...] = cotb[k].astype(F32).reshape(4 * 32 * ROWS, 128)
        for q in range(2):

            def chunk(ci, _):
                u = jnp.dot(
                    ak[p, q], stacked(near, far, q, ci * 512, 512), preferred_element_type=F32
                )
                for j in range(4):
                    n = ci * 4 + j
                    taps = [u[32 * c:32 * c + 32, 128 * j:128 * j + 128] for c in range(4)]
                    pre = (taps[1] + up(taps[3]), taps[2] + down(taps[0]))
                    grads = []
                    for s in range(2):
                        rows = pl.ds((2 * q + s) * 32 * ROWS + n, 32, stride=ROWS)
                        sig = 0.5 * jnp.tanh(0.5 * pre[s]) + 0.5
                        act = pre[s] * sig
                        actf[rows, :] = act
                        grads.append(cotf[rows, :] * (sig + act * (1.0 - sig)))
                    four = (up(grads[1]), grads[0], grads[1], down(grads[0]))
                    g_s[p, q, m, :, lanes((n + 2) * 128, 128)] = jnp.concatenate(
                        [value.astype(BF) for value in four], axis=0
                    )
                return 0

            lax.fori_loop(0, ROWS // 4, chunk, 0)

            def grad(ci, total):
                return total + nt_dot(
                    g_s[p, q, m, :, lanes((2 + 4 * ci) * 128, 512)],
                    stacked(near, far, q, ci * 512, 512),
                )

            start = jnp.zeros((128, 256), F32) if k < 2 else w_s[p, q]
            w_s[p, q] = lax.fori_loop(0, ROWS // 4, grad, start)
        actb[k] = actf[...].reshape(4, 32, ROWS, 128).astype(BF)
        copy = pltpu.make_async_copy(actb.at[k], act_ref.at[pl.ds(4 * p, 4), :, m], o_sem.at[k])
        copy.start()
        return copy

    ysends[0].wait_recv()
    ysends[1].wait_recv()

    @pl.when(first_y)
    def _():
        vt[own, :, low] = jnp.zeros((2, 64, 128), BF)

    @pl.when(last_y)
    def _():
        vt[own, :, high] = jnp.zeros((2, 64, 128), BF)

    outs = [block(0), block(1)]

    def halo(index, slot):
        sends[index].wait_recv()
        turn_in(lambda: face[index], slot)
        sends[4 + 2 * index].wait_recv()
        sends[5 + 2 * index].wait_recv()

        @pl.when(first_y)
        def _():
            vt[slot, :, low] = jnp.zeros((64, 128), BF)

        @pl.when(last_y)
        def _():
            vt[slot, :, high] = jnp.zeros((64, 128), BF)

    halo(1, 3 - 3 * core)
    outs.append(block(2))
    w_send[...] = w_s[other].reshape(256, 256).astype(BF)
    swap = remote(w_send, w_recv, ws.at[0], wr.at[0], neighbours[1])
    swap.start()

    halo(0, 3 * core)

    @pl.when(no_far)
    def _():
        vt[3 * core] = jnp.zeros((64, HALO), BF)

    outs.append(block(3))

    swap.wait_recv()
    w_s[core] = w_s[core] + w_recv[...].astype(F32).reshape(2, 128, 256)
    w_bf[...] = w_s[core].reshape(256, 256).astype(BF)
    scatter = []
    for i in range(1, 16):
        index, peer = plane_peer(i)
        scatter.append(remote(w_bf.at[pl.ds(pl.multiple_of(16 * index, 16), 16)], rs_in.at[i], ws.at[1], wr.at[1], peer))
    for copy in scatter:
        copy.start()

    def back(target, terms, ci):
        total = None
        for a, p, m in terms:
            parts = [
                g_s[p, BACK[b][0], m, :, lanes((ci * 6 + 1 + BACK[b][1]) * 128, 768)]
                for b in range(4)
            ]
            product = jnp.dot(bk[a], jnp.concatenate(parts, axis=0), preferred_element_type=F32)
            total = product if total is None else total + product
        return total

    def outer(ci, _):
        igb[0, :, lanes(ci * 768, 768)] = back(0, ((3, 0, 0),), ci).astype(BF)
        igb[1, :, lanes(ci * 768, 768)] = back(3, ((0, 1, 1),), ci).astype(BF)
        return 0

    lax.fori_loop(0, 3, outer, 0)
    body = pl.ds(128, WIDE)
    bsends = [
        remote(igb.at[core, :, body], rx.at[0], bs.at[0], br.at[0], neighbours[0]),
        remote(igb.at[other, :, body], rx.at[1], bs.at[1], br.at[1], neighbours[1]),
    ]
    for copy in bsends:
        copy.start()

    def inner(ci, _):
        igf[0, :, lanes(ci * 768, 768)] = back(1, ((1, 0, 0), (2, 1, 0), (3, 0, 1)), ci)
        igf[1, :, lanes(ci * 768, 768)] = back(2, ((1, 0, 1), (2, 1, 1), (0, 1, 0)), ci)
        return 0

    lax.fori_loop(0, 3, inner, 0)
    igy[0] = igf[:, :, 0:128].astype(BF)
    igy[1] = igf[:, :, HALO - 128:].astype(BF)
    for k in range(2):
        bsends.append(remote(igy.at[k], ry.at[k], bs.at[2 + k], br.at[2 + k], neighbours[2 + k]))
    for index, m in ((0, core), (1, other)):
        for k, part_lanes in enumerate((low, high)):
            at = 4 + 2 * index + k
            bsends.append(remote(igb.at[m, :, part_lanes], rc.at[index, k], bs.at[at], br.at[at], neighbours[at]))
    for copy in bsends[2:]:
        copy.start()

    mine = 4 * x + y
    remote(w_bf.at[pl.ds(0, 240)].reshape(15, 16, 256), rs_in.at[pl.ds(1, 15)], ws.at[1], wr.at[1], neighbours[1]).wait_recv()
    q = mine // 8
    total = w_s[core, q, pl.ds(pl.multiple_of(16 * lax.rem(mine, 8), 16), 16)]
    for i in range(1, 16):
        total = total + rs_in[i].astype(F32)
    part[...] = total
    z_in[z] = total
    gather_z = [remote(part, z_in.at[z], ws.at[2], wr.at[2], z_peer(i)) for i in range(1, 4)]
    for copy in gather_z:
        copy.start()
    three = z_in.at[pl.ds(0, 3)]
    remote(three, three, ws.at[2], wr.at[2], neighbours[1]).wait_recv()
    total = (z_in[0] + z_in[1]) + (z_in[2] + z_in[3])
    fin[core, pl.ds(pl.multiple_of(16 * mine, 16), 16)] = (total * scaling).astype(BF)
    spread = []
    for i in range(1, 16):
        _, peer = plane_peer(i)
        shard = fin.at[core, pl.ds(pl.multiple_of(16 * mine, 16), 16)]
        spread.append(remote(shard, shard, ws.at[3], wr.at[3], peer))
    for copy in spread:
        copy.start()

    def add(index, k, src, m, keep):
        place = (128, ROWS * 128)[k]

        @pl.when(keep)
        def _():
            igf[m, :, pl.ds(place, 128)] = igf[m, :, pl.ds(place, 128)] + src().astype(F32)

    bsends[2].wait_recv()
    bsends[3].wait_recv()
    for m in range(2):
        add(2, 1, lambda m=m: ry[0, m], m, jnp.logical_not(last_y))
        add(3, 0, lambda m=m: ry[1, m], m, jnp.logical_not(first_y))
    for index, m in ((1, other), (0, core)):
        ok = jnp.logical_not(no_far) if index == 0 else True
        bsends[index].wait_recv()
        bsends[4 + 2 * index].wait_recv()
        bsends[5 + 2 * index].wait_recv()

        def add_face(index=index, m=m):
            igf[m, :, body] = igf[m, :, body] + rx[index].astype(F32)

        if index == 0:
            pl.when(ok)(add_face)
        else:
            add_face()
        add(4, 1, lambda index=index: rc[index, 0], m, jnp.logical_and(ok, jnp.logical_not(last_y)))
        add(5, 0, lambda index=index: rc[index, 1], m, jnp.logical_and(ok, jnp.logical_not(first_y)))
        for n in range(ROWS):
            turn[pl.ds(n, 64, stride=ROWS), :] = igf[m, :, pl.ds((n + 1) * 128, 128)]
        igo[:, m] = turn[...].reshape(64, ROWS, 128).astype(BF)
    ig_copy = pltpu.make_async_copy(igo, ig_ref, o_sem.at[4])
    ig_copy.start()
    outs.append(ig_copy)

    remote(w_bf.at[pl.ds(0, 240)], fin.at[core, pl.ds(0, 240)], ws.at[3], wr.at[3], neighbours[1]).wait_recv()
    both = remote(fin.at[core], fin.at[core], ws.at[4], wr.at[4], neighbours[1])
    both.start()
    both.wait_recv()
    for p in range(2):
        for q in range(2):
            for i, (a, b) in enumerate([(a, b) for a in (1 + p, 3 - 3 * p) for b in (1 + q, 3 - 3 * q)]):
                value = fin[p, 128 * q:128 * q + 128, 64 * i:64 * i + 64]
                wgo[a, b] = value.astype(F32).reshape(4, 32, 64)
    wg_copy = pltpu.make_async_copy(wgo, wg_ref, o_sem.at[5])
    wg_copy.start()
    outs.append(wg_copy)

    for copy in sends + bsends + [swap, both]:
        copy.wait_send()
    remote(three, three, ws.at[2], wr.at[2], neighbours[1]).wait_send()
    remote(w_bf.at[pl.ds(0, 240)], fin.at[core, pl.ds(0, 240)], ws.at[1], wr.at[1], neighbours[1]).wait_send()
    remote(w_bf.at[pl.ds(0, 240)], fin.at[core, pl.ds(0, 240)], ws.at[3], wr.at[3], neighbours[1]).wait_send()
    for copy in outs:
        copy.wait()


def on_device(volume, kernel, cotangent):
    cells = volume.shape[1] * volume.shape[2] * volume.shape[3]
    scaling = 1.0 / math.sqrt(cells * lax.axis_size("gx") * lax.axis_size("gy"))
    anywhere = pl.BlockSpec(memory_space=pl.ANY)
    inside = pl.BlockSpec(memory_space=pltpu.VMEM)
    dma = pltpu.SemaphoreType.DMA
    act, ig, wg = pl.pallas_call(
        functools.partial(step_kernel, scaling),
        out_shape=(
            jax.ShapeDtypeStruct((8, 32, 2, ROWS, 128), BF),
            jax.ShapeDtypeStruct((64, 2, ROWS, 128), BF),
            jax.ShapeDtypeStruct((4, 4, 4, 32, 64), F32),
        ),
        in_specs=[anywhere, inside, anywhere],
        out_specs=(anywhere, anywhere, anywhere),
        scratch_shapes=[
            pltpu.VMEM((64, 2, ROWS, 128), BF),
            pltpu.VMEM((2, 64, ROWS, 128), BF),
            pltpu.VMEM((64 * ROWS, 128), F32),
            pltpu.VMEM((4, 64, HALO), BF),
            pltpu.VMEM((4, 4, 32, ROWS, 128), BF),
            pltpu.VMEM((4 * 32 * ROWS, 128), F32),
            pltpu.VMEM((4 * 32 * ROWS, 128), F32),
            pltpu.VMEM((4, 4, 32, ROWS, 128), BF),
            pltpu.VMEM((2, 2, 2, 128, (ROWS + 4) * 128), BF),
            pltpu.VMEM((2, 2, 128, 256), BF),
            pltpu.VMEM((4, 64, 512), BF),
            pltpu.VMEM((2, 2, 128, 256), F32),
            pltpu.VMEM((256, 256), BF),
            pltpu.VMEM((256, 256), BF),
            pltpu.VMEM((256, 256), BF),
            pltpu.VMEM((16, 16, 256), BF),
            pltpu.VMEM((16, 256), F32),
            pltpu.VMEM((4, 16, 256), F32),
            pltpu.VMEM((2, 256, 256), BF),
            pltpu.VMEM((2, 64, HALO), F32),
            pltpu.VMEM((2, 64, HALO), BF),
            pltpu.VMEM((2, 2, 64, 128), BF),
            pltpu.VMEM((2, 64, WIDE), BF),
            pltpu.VMEM((2, 2, 64, 128), BF),
            pltpu.VMEM((2, 2, 64, 128), BF),
            pltpu.VMEM((64, 2, ROWS, 128), BF),
            pltpu.VMEM((4, 4, 4, 32, 64), F32),
            dma((5,)), dma((6,)), dma((8,)), dma((8,)), dma((8,)), dma((8,)), dma((5,)), dma((5,)),
        ],
        compiler_params=pltpu.CompilerParams(
            collective_id=0, has_side_effects=True, vmem_limit_bytes=60 * 1024 * 1024
        ),
        name="conv_step",
    )(volume, kernel, cotangent.reshape(8, 32, 2, ROWS, 128))
    return act.reshape(2, 2, 2, 32, 2, ROWS, 128), ig, wg


def solution(mesh):
    placed = (P(None, "gx", "gy", None), P(), P(None, None, None, None, "gx", "gy", None))
    return jax.shard_map(
        on_device,
        mesh=mesh,
        in_specs=placed,
        out_specs=(P(None, None, None, None, "gx", "gy", None), P(None, "gx", "gy", None), P()),
        check_vma=False,
    )
```

time: 346 us -> 61.4 us (0.18)
  waiting for transfers between devices: 159 us -> 0 us
  matrix products: 114 us -> 0 us
  Pallas kernels: 0 us -> 55.4 us
  starting transfers between devices: 21.2 us -> 0 us
  other arithmetic: 15.5 us -> 0 us
  between operations: 15.3 us -> 0.66 us
  local copies, waits for them, and re-layouts: 17.6 us -> 5.16 us
    psum x1 -> x0, waiting for transfers between devices: 125 us -> none  [on_device(): stacked_grad = lax.psum(stacked_grad, ('gx', 'gy'))]
    dot_general x192 -> x0, matrix products: 114 us -> none  [the longest x64 75.5 us: on_device(): lax.dot_general(kernel[tap_x, tap_y, tap_z], piece, (((0,), (0,)), ((), (...]
    pallas_call x0 -> x1, Pallas kernels: none -> 55.4 us  [on_device(): pl.pallas_call(functools.partial(step_kernel, scaling), out_shape=(jax.Sh...]
    ppermute x8 -> x0, waiting for transfers between devices: 34.2 us -> none  [the longest x4 23.8 us: padded_2(): lax.ppermute(lax.slice_in_dim(block, block.shape[dim] - width, None, axis...]
    ppermute x8 -> x0, starting transfers between devices: 21.2 us -> none  [the longest x4 14.8 us: padded_2(): lax.ppermute(lax.slice_in_dim(block, block.shape[dim] - width, None, axis...]
    unnamed x111 -> x7, local copies, waits for them, and re-layouts: 15.9 us -> 5.16 us
    concatenate x3 -> x0, other arithmetic: 10.7 us -> none  [padded_2(): block = jnp.concatenate([low, block, high], axis=dim)]
  transfers between devices with their start and end apart: 9 -> 0, of which waited for: 5 -> 0; matrix products, arithmetic and copies ran while one was open for 7% -> 0% of each run, Pallas kernels for 0% -> 0%
where the time goes in v1:
time: 61.4 us; the launch traced here: 61.2 us
  Pallas kernels  55.4 us (90%)
  local copies, waits for them, and re-layouts  5.16 us (8%)
  between operations  0.66 us (1%)
    pallas_call x1, Pallas kernels, on_device(): pl.pallas_call(functools.partial(step_kernel, scaling), out_shape=(jax.Sh...  55.4 us
    unnamed x7, local copies, waits for them, and re-layouts  5.16 us

profile of v1, /device:TPU:1, one launch (start us, length us, event | category | flops | bytes accessed | tf_op | source)
XLA Modules:
  0.0 61.2 jit_solution(13805530103982283357)
XLA Ops:
  0.6 55.4 %conv_step.1 = (bf16[8,32,2,16,128]{4,3,2,1,0:T(8,128)(2,1)}, bf16[64,2,16,128]{3,2,1,0:T(8,128)(2,1)}, f32[4,4,4,32,64]{4,3,2,1,0:T(8,128)}) custom-call(bf16[64,2,16,128]{3,2,1,0:T(8,128)(2,1)} %vol_ref.1, bf16[4,4,4,32,64]{4,3,2,1,0:T(8,128)(2,1)} %ker_ref.1, bf16[8,32,2,16,128]{4,3,2,1,0:T(8,128)(2,1)} %bitcast.2), custom_call_target="tpu_custom_call" | custom-call | tf_op jit(solution)/shard_map/conv_step/pallas_call | solution.py:374
  56.1 0.0 copy-start.1
  56.1 0.0 copy-start
  56.1 3.4 %copy.9 = bf16[2,2,2,32,2,16,128]{6,5,4,3,2,1,0:T(8,128)(2,1)} copy(bf16[2,2,2,32,2,16,128]{6,5,4,3,2,1,0:T(8,128)(2,1)} %bitcast.3) | data formatting | bytes 4194304
  59.5 0.0 copy-done.1
  59.5 0.8 %copy.10 = bf16[64,2,16,128]{3,2,1,0:T(8,128)(2,1)} copy(bf16[64,2,16,128]{3,2,1,0:T(8,128)(2,1)S(1)} %copy-done.1) | data formatting | bytes 1048576
  60.3 0.0 copy-done
  60.3 1.0 %copy.11 = f32[4,4,4,32,64]{4,3,2,1,0:T(8,128)} copy(f32[4,4,4,32,64]{4,3,2,1,0:T(8,128)S(1)} %copy-done) | data formatting | bytes 1048576
Async XLA Ops:
  56.1 3.4 %copy-start.1 = (bf16[64,2,16,128]{3,2,1,0:T(8,128)(2,1)S(1)}, bf16[64,2,16,128]{3,2,1,0:T(8,128)(2,1)}, u32[]{:S(2)}) copy-start(bf16[64,2,16,128]{3,2,1,0:T(8,128)(2,1)} %get-tuple-element.13) | copy-start | bytes 1572868
  56.1 4.2 %copy-start = (f32[4,4,4,32,64]{4,3,2,1,0:T(8,128)S(1)}, f32[4,4,4,32,64]{4,3,2,1,0:T(8,128)}, u32[]{:S(2)}) copy-start(f32[4,4,4,32,64]{4,3,2,1,0:T(8,128)} %get-tuple-element.14) | copy-start | bytes 1572868

commit v2 on v1

--- a/solution.py
+++ b/solution.py
@@ -33,11 +33,11 @@
 
 
 def step_kernel(
-    scaling, vol_ref, ker_ref, cot_ref, act_ref, ig_ref, wg_ref,
-    volb, face, turn, vt, cotb, cotf, actf, actb, g_s, ak, bk, w_s,
-    w_send, w_recv, w_bf, rs_in, part, z_in, fin,
-    igf, igb, igy, rx, ry, rc, igo, wgo,
-    l_sem, o_sem, fs, fr, bs, br, ws, wr,
+    scaling, vol_ref, ker_hbm, cot_ref, act_ref, igo, fin,
+    volb, ker_ref, face, turn, vt, cotb, cotf, actf, ua, ub, g_s, ak, bk, w_s,
+    w_send, w_recv, w_bf, rs_in, part, z_in,
+    igf, igb, igy, rx, ry, rc,
+    l_sem, fs, fr, bs, br, ws, wr,
 ):
     gx, gy = lax.axis_index("gx"), lax.axis_index("gy")
     core = lax.rem(gx, 2)
@@ -67,6 +67,8 @@
 
     vol_copy = pltpu.make_async_copy(vol_ref, volb, l_sem.at[4])
     vol_copy.start()
+    ker_copy = pltpu.make_async_copy(ker_hbm, ker_ref, l_sem.at[5])
+    ker_copy.start()
     blocks = [(1, 0), (0, 1), (other, other), (core, core)]
     cot_copies = []
     for k, (p, m) in enumerate(blocks):
@@ -80,6 +82,44 @@
     for peer in peers:
         pl.semaphore_signal(barrier, inc=1, device_id=peer, device_id_type=MESH)
 
+    def turn_in(get, slot):
+        turn[...] = get().astype(F32).reshape(64 * ROWS, 128)
+
+        def row(n, _):
+            vt[slot, :, lanes((n + 1) * 128, 128)] = turn[pl.ds(n, 64, stride=ROWS), :].astype(BF)
+            return 0
+
+        lax.fori_loop(0, ROWS, row, 0, unroll=True)
+
+    vol_copy.wait()
+    turn_in(lambda: volb[:, 0], 1)
+    turn_in(lambda: volb[:, 1], 2)
+    pl.semaphore_wait(barrier, len(peers))
+
+    sends = [
+        remote(volb.at[:, core], face.at[0], fs.at[0], fr.at[0], neighbours[0]),
+        remote(volb.at[:, other], face.at[1], fs.at[1], fr.at[1], neighbours[1]),
+    ]
+    for copy in sends:
+        copy.start()
+
+    first, last = pl.ds(128, 128), pl.ds(ROWS * 128, 128)
+    low, high = pl.ds(0, 128), pl.ds((ROWS + 1) * 128, 128)
+    own = pl.ds(1, 2)
+    ysends = [
+        remote(vt.at[own, :, first], vt.at[own, :, high], fs.at[2], fr.at[2], neighbours[2]),
+        remote(vt.at[own, :, last], vt.at[own, :, low], fs.at[3], fr.at[3], neighbours[3]),
+    ]
+    for k, (m, slot) in enumerate(((core, 3 - 3 * core), (other, 3 * core))):
+        base = 4 + 2 * k
+        ysends.append(remote(vt.at[1 + m, :, first], vt.at[slot, :, high], fs.at[base], fr.at[base], neighbours[base]))
+        ysends.append(remote(vt.at[1 + m, :, last], vt.at[slot, :, low], fs.at[base + 1], fr.at[base + 1], neighbours[base + 1]))
+    for copy in ysends:
+        copy.start()
+    sends += ysends
+
+    half = jnp.asarray(0.5, BF)
+    ker_copy.wait()
     for p in range(2):
         for q in range(2):
             pieces = [
@@ -87,48 +127,12 @@
                 for a in (1 + p, 3 - 3 * p)
                 for b in (1 + q, 3 - 3 * q)
             ]
-            ak[p, q] = jnp.concatenate(pieces, axis=1)
+            ak[p, q] = jnp.concatenate(pieces, axis=1) * half
     for a in range(4):
-        bk[a] = ker_ref[a].reshape(512, 64).astype(F32).T.astype(BF)
+        bk[a] = ker_ref[a].reshape(512, 64).astype(F32).T.astype(BF) * half
     g_s[:, :, :, :, 0:256] = jnp.zeros((2, 2, 2, 128, 256), BF)
     g_s[:, :, :, :, 256 + WIDE:] = jnp.zeros((2, 2, 2, 128, 256), BF)
 
-    vol_copy.wait()
-    pl.semaphore_wait(barrier, len(peers))
-
-    sends = [
-        remote(volb.at[:, core], face.at[0], fs.at[0], fr.at[0], neighbours[0]),
-        remote(volb.at[:, other], face.at[1], fs.at[1], fr.at[1], neighbours[1]),
-    ]
-    for copy in sends:
-        copy.start()
-
-    def turn_in(get, slot):
-        turn[...] = get().astype(F32).reshape(64 * ROWS, 128)
-
-        def row(n, _):
-            vt[slot, :, lanes((n + 1) * 128, 128)] = turn[pl.ds(n, 64, stride=ROWS), :].astype(BF)
-            return 0
-
-        lax.fori_loop(0, ROWS, row, 0, unroll=True)
-
-    turn_in(lambda: volb[:, 0], 1)
-    turn_in(lambda: volb[:, 1], 2)
-
-    first, last = pl.ds(128, 128), pl.ds(ROWS * 128, 128)
-    low, high = pl.ds(0, 128), pl.ds((ROWS + 1) * 128, 128)
-    own = pl.ds(1, 2)
-    ysends = [
-        remote(vt.at[own, :, first], vt.at[own, :, high], fs.at[2], fr.at[2], neighbours[2]),
-        remote(vt.at[own, :, last], vt.at[own, :, low], fs.at[3], fr.at[3], neighbours[3]),
-    ]
-    for k, (m, slot) in enumerate(((core, 3 - 3 * core), (other, 3 * core))):
-        base = 4 + 2 * k
-        ysends.append(remote(vt.at[1 + m, :, first], vt.at[slot, :, high], fs.at[base], fr.at[base], neighbours[base]))
-        ysends.append(remote(vt.at[1 + m, :, last], vt.at[slot, :, low], fs.at[base + 1], fr.at[base + 1], neighbours[base + 1]))
-    for copy in ysends:
-        copy.start()
-    sends += ysends
 
     lane = lax.broadcasted_iota(jnp.int32, (32, 128), 1)
 
@@ -155,43 +159,46 @@
         near, far = m + 1, m + 2 * p
         cot_copies[k].wait()
         cotf[...] = cotb[k].astype(F32).reshape(4 * 32 * ROWS, 128)
+
+        def product(t, dst):
+            q, ci = t // 4, lax.rem(t, 4)
+            dst[...] = jnp.dot(
+                ak[p, q], stacked(near, far, q, ci * 512, 512), preferred_element_type=F32
+            )
+
+        def finish(t, src):
+            q, ci = t // 4, lax.rem(t, 4)
+            for j in range(4):
+                n = ci * 4 + j
+                taps = [src[32 * c:32 * c + 32, 128 * j:128 * j + 128] for c in range(4)]
+                halves = (taps[1] + up(taps[3]), taps[2] + down(taps[0]))
+                grads = []
+                for s in range(2):
+                    rows = pl.ds((2 * q + s) * 32 * ROWS + n, 32, stride=ROWS)
+                    t_h = jnp.tanh(halves[s])
+                    w = 1.0 + t_h
+                    act = halves[s] * w
+                    actf[rows, :] = act
+                    grads.append(cotf[rows, :] * (w + act * (1.0 - t_h)))
+                four = (up(grads[1]), grads[0], grads[1], down(grads[0]))
+                g_s[p, q, m, :, lanes((n + 2) * 128, 128)] = jnp.concatenate(
+                    [value.astype(BF) for value in four], axis=0
+                )
+
+        product(0, ua)
+
+        def pair(i, _):
+            product(2 * i + 1, ub)
+            finish(2 * i, ua)
+            product(jnp.minimum(2 * i + 2, 7), ua)
+            finish(2 * i + 1, ub)
+            return 0
+
+        lax.fori_loop(0, 4, pair, 0)
         for q in range(2):
-
-            def chunk(ci, _):
-                u = jnp.dot(
-                    ak[p, q], stacked(near, far, q, ci * 512, 512), preferred_element_type=F32
-                )
-                for j in range(4):
-                    n = ci * 4 + j
-                    taps = [u[32 * c:32 * c + 32, 128 * j:128 * j + 128] for c in range(4)]
-                    pre = (taps[1] + up(taps[3]), taps[2] + down(taps[0]))
-                    grads = []
-                    for s in range(2):
-                        rows = pl.ds((2 * q + s) * 32 * ROWS + n, 32, stride=ROWS)
-                        sig = 0.5 * jnp.tanh(0.5 * pre[s]) + 0.5
-                        act = pre[s] * sig
-                        actf[rows, :] = act
-                        grads.append(cotf[rows, :] * (sig + act * (1.0 - sig)))
-                    four = (up(grads[1]), grads[0], grads[1], down(grads[0]))
-                    g_s[p, q, m, :, lanes((n + 2) * 128, 128)] = jnp.concatenate(
-                        [value.astype(BF) for value in four], axis=0
-                    )
-                return 0
-
-            lax.fori_loop(0, ROWS // 4, chunk, 0)
-
-            def grad(ci, total):
-                return total + nt_dot(
-                    g_s[p, q, m, :, lanes((2 + 4 * ci) * 128, 512)],
-                    stacked(near, far, q, ci * 512, 512),
-                )
-
-            start = jnp.zeros((128, 256), F32) if k < 2 else w_s[p, q]
-            w_s[p, q] = lax.fori_loop(0, ROWS // 4, grad, start)
-        actb[k] = actf[...].reshape(4, 32, ROWS, 128).astype(BF)
-        copy = pltpu.make_async_copy(actb.at[k], act_ref.at[pl.ds(4 * p, 4), :, m], o_sem.at[k])
-        copy.start()
-        return copy
+            grad = nt_dot(g_s[p, q, m, :, 256:256 + WIDE], stacked(near, far, q, 0, WIDE))
+            w_s[p, q] = grad if k < 2 else w_s[p, q] + grad
+        act_ref[pl.ds(4 * p, 4), :, m] = actf[...].reshape(4, 32, ROWS, 128).astype(BF)
 
     ysends[0].wait_recv()
     ysends[1].wait_recv()
@@ -204,7 +211,8 @@
     def _():
         vt[own, :, high] = jnp.zeros((2, 64, 128), BF)
 
-    outs = [block(0), block(1)]
+    block(0)
+    block(1)
 
     def halo(index, slot):
         sends[index].wait_recv()
@@ -221,7 +229,7 @@
             vt[slot, :, high] = jnp.zeros((64, 128), BF)
 
     halo(1, 3 - 3 * core)
-    outs.append(block(2))
+    block(2)
     w_send[...] = w_s[other].reshape(256, 256).astype(BF)
     swap = remote(w_send, w_recv, ws.at[0], wr.at[0], neighbours[1])
     swap.start()
@@ -232,7 +240,7 @@
     def _():
         vt[3 * core] = jnp.zeros((64, HALO), BF)
 
-    outs.append(block(3))
+    block(3)
 
     swap.wait_recv()
     w_s[core] = w_s[core] + w_recv[...].astype(F32).reshape(2, 128, 256)
@@ -300,7 +308,7 @@
     three = z_in.at[pl.ds(0, 3)]
     remote(three, three, ws.at[2], wr.at[2], neighbours[1]).wait_recv()
     total = (z_in[0] + z_in[1]) + (z_in[2] + z_in[3])
-    fin[core, pl.ds(pl.multiple_of(16 * mine, 16), 16)] = (total * scaling).astype(BF)
+    fin[core, pl.ds(pl.multiple_of(16 * mine, 16), 16)] = (total * (0.5 * scaling)).astype(BF)
     spread = []
     for i in range(1, 16):
         _, peer = plane_peer(i)
@@ -339,56 +347,68 @@
         for n in range(ROWS):
             turn[pl.ds(n, 64, stride=ROWS), :] = igf[m, :, pl.ds((n + 1) * 128, 128)]
         igo[:, m] = turn[...].reshape(64, ROWS, 128).astype(BF)
-    ig_copy = pltpu.make_async_copy(igo, ig_ref, o_sem.at[4])
-    ig_copy.start()
-    outs.append(ig_copy)
 
     remote(w_bf.at[pl.ds(0, 240)], fin.at[core, pl.ds(0, 240)], ws.at[3], wr.at[3], neighbours[1]).wait_recv()
     both = remote(fin.at[core], fin.at[core], ws.at[4], wr.at[4], neighbours[1])
     both.start()
     both.wait_recv()
-    for p in range(2):
-        for q in range(2):
-            for i, (a, b) in enumerate([(a, b) for a in (1 + p, 3 - 3 * p) for b in (1 + q, 3 - 3 * q)]):
-                value = fin[p, 128 * q:128 * q + 128, 64 * i:64 * i + 64]
-                wgo[a, b] = value.astype(F32).reshape(4, 32, 64)
-    wg_copy = pltpu.make_async_copy(wgo, wg_ref, o_sem.at[5])
-    wg_copy.start()
-    outs.append(wg_copy)
-
     for copy in sends + bsends + [swap, both]:
         copy.wait_send()
     remote(three, three, ws.at[2], wr.at[2], neighbours[1]).wait_send()
     remote(w_bf.at[pl.ds(0, 240)], fin.at[core, pl.ds(0, 240)], ws.at[1], wr.at[1], neighbours[1]).wait_send()
     remote(w_bf.at[pl.ds(0, 240)], fin.at[core, pl.ds(0, 240)], ws.at[3], wr.at[3], neighbours[1]).wait_send()
-    for copy in outs:
+
+
+def write_kernel(act, ig, fin, act_ref, ig_ref, wg_ref, wgo, sem):
+    copies = [
+        pltpu.make_async_copy(act.at[pl.ds(2 * i, 2)], act_ref.at[pl.ds(2 * i, 2)], sem.at[i])
+        for i in range(4)
+    ]
+    copies.append(pltpu.make_async_copy(ig, ig_ref, sem.at[4]))
+    for copy in copies:
+        copy.start()
+    for p in range(2):
+        for q in range(2):
+            taps = [(a, b) for a in (1 + p, 3 - 3 * p) for b in (1 + q, 3 - 3 * q)]
+            for i, (a, b) in enumerate(taps):
+                value = fin[p, 128 * q:128 * q + 128, 64 * i:64 * i + 64]
+                wgo[a, b] = value.astype(F32).reshape(4, 32, 64)
+    copies.append(pltpu.make_async_copy(wgo, wg_ref, sem.at[5]))
+    copies[-1].start()
+    for copy in copies:
         copy.wait()
 
 
 def on_device(volume, kernel, cotangent):
     cells = volume.shape[1] * volume.shape[2] * volume.shape[3]
     scaling = 1.0 / math.sqrt(cells * lax.axis_size("gx") * lax.axis_size("gy"))
-    anywhere = pl.BlockSpec(memory_space=pl.ANY)
+    anywhere = pl.BlockSpec(memory_space=pltpu.HBM)
     inside = pl.BlockSpec(memory_space=pltpu.VMEM)
     dma = pltpu.SemaphoreType.DMA
-    act, ig, wg = pl.pallas_call(
+    operands = [
+        pltpu.with_memory_space_constraint(value, pltpu.HBM)
+        for value in (volume, kernel, cotangent.reshape(8, 32, 2, ROWS, 128))
+    ]
+    results = pl.pallas_call(
         functools.partial(step_kernel, scaling),
         out_shape=(
-            jax.ShapeDtypeStruct((8, 32, 2, ROWS, 128), BF),
-            jax.ShapeDtypeStruct((64, 2, ROWS, 128), BF),
-            jax.ShapeDtypeStruct((4, 4, 4, 32, 64), F32),
+            pltpu.VMEM((8, 32, 2, ROWS, 128), BF),
+            pltpu.VMEM((64, 2, ROWS, 128), BF),
+            pltpu.VMEM((2, 256, 256), BF),
         ),
-        in_specs=[anywhere, inside, anywhere],
-        out_specs=(anywhere, anywhere, anywhere),
+        in_specs=[anywhere, anywhere, anywhere],
+        out_specs=(inside, inside, inside),
         scratch_shapes=[
             pltpu.VMEM((64, 2, ROWS, 128), BF),
+            pltpu.VMEM((4, 4, 4, 32, 64), BF),
             pltpu.VMEM((2, 64, ROWS, 128), BF),
             pltpu.VMEM((64 * ROWS, 128), F32),
             pltpu.VMEM((4, 64, HALO), BF),
             pltpu.VMEM((4, 4, 32, ROWS, 128), BF),
             pltpu.VMEM((4 * 32 * ROWS, 128), F32),
             pltpu.VMEM((4 * 32 * ROWS, 128), F32),
-            pltpu.VMEM((4, 4, 32, ROWS, 128), BF),
+            pltpu.VMEM((128, 512), F32),
+            pltpu.VMEM((128, 512), F32),
             pltpu.VMEM((2, 2, 2, 128, (ROWS + 4) * 128), BF),
             pltpu.VMEM((2, 2, 128, 256), BF),
             pltpu.VMEM((4, 64, 512), BF),
@@ -399,22 +419,33 @@
             pltpu.VMEM((16, 16, 256), BF),
             pltpu.VMEM((16, 256), F32),
             pltpu.VMEM((4, 16, 256), F32),
-            pltpu.VMEM((2, 256, 256), BF),
             pltpu.VMEM((2, 64, HALO), F32),
             pltpu.VMEM((2, 64, HALO), BF),
             pltpu.VMEM((2, 2, 64, 128), BF),
             pltpu.VMEM((2, 64, WIDE), BF),
             pltpu.VMEM((2, 2, 64, 128), BF),
             pltpu.VMEM((2, 2, 64, 128), BF),
-            pltpu.VMEM((64, 2, ROWS, 128), BF),
-            pltpu.VMEM((4, 4, 4, 32, 64), F32),
-            dma((5,)), dma((6,)), dma((8,)), dma((8,)), dma((8,)), dma((8,)), dma((5,)), dma((5,)),
+            dma((6,)), dma((8,)), dma((8,)), dma((8,)), dma((8,)), dma((5,)), dma((5,)),
         ],
         compiler_params=pltpu.CompilerParams(
-            collective_id=0, has_side_effects=True, vmem_limit_bytes=60 * 1024 * 1024
+            collective_id=0, has_side_effects=True, vmem_limit_bytes=40 * 1024 * 1024
         ),
         name="conv_step",
-    )(volume, kernel, cotangent.reshape(8, 32, 2, ROWS, 128))
+    )(*operands)
+    results = [pltpu.with_memory_space_constraint(value, pltpu.VMEM) for value in results]
+    act, ig, wg = pl.pallas_call(
+        write_kernel,
+        out_shape=(
+            jax.ShapeDtypeStruct((8, 32, 2, ROWS, 128), BF),
+            jax.ShapeDtypeStruct((64, 2, ROWS, 128), BF),
+            jax.ShapeDtypeStruct((4, 4, 4, 32, 64), F32),
+        ),
+        in_specs=[inside] * 3,
+        out_specs=(anywhere,) * 3,
+        scratch_shapes=[pltpu.VMEM((4, 4, 4, 32, 64), F32), dma((6,))],
+        compiler_params=pltpu.CompilerParams(vmem_limit_bytes=16 * 1024 * 1024),
+        name="write_out",
+    )(*results)
     return act.reshape(2, 2, 2, 32, 2, ROWS, 128), ig, wg
 
 

time: 61.4 us -> 46.9 us (0.76)
  Pallas kernels: 55.4 us -> 46.1 us
  local copies, waits for them, and re-layouts: 5.16 us -> 0 us
    pallas_call x1 -> x2, Pallas kernels: 55.4 us -> 46.1 us  [the longest x1 44.3 us: on_device(): pl.pallas_call(functools.partial(step_kernel, scaling), out_shape=(pltpu....]
    unnamed x7 -> x0, local copies, waits for them, and re-layouts: 5.16 us -> none
where the time goes in v2:
time: 46.9 us; the launch traced here: 46.8 us
  Pallas kernels  46.1 us (98%)
  between operations  0.64 us (1%)
    pallas_call x1, Pallas kernels, on_device(): pl.pallas_call(functools.partial(step_kernel, scaling), out_shape=(pltpu....  44.3 us
    pallas_call x1, Pallas kernels, on_device(): pl.pallas_call(write_kernel, out_shape=(jax.ShapeDtypeStruct((8, 32, 2, R...  1.89 us

profile of v2, /device:TPU:1, one launch (start us, length us, event | category | flops | bytes accessed | tf_op | source)
XLA Modules:
  0.0 46.8 jit_solution(1703907750863807836)
XLA Ops:
  0.6 44.3 %conv_step.1 = (bf16[8,32,2,16,128]{4,3,2,1,0:T(8,128)(2,1)S(1)}, bf16[64,2,16,128]{3,2,1,0:T(8,128)(2,1)S(1)}, bf16[2,256,256]{2,1,0:T(8,128)(2,1)S(1)}) custom-call(bf16[64,2,16,128]{3,2,1,0:T(8,128)(2,1)} %vol_ref.1, bf16[4,4,4,32,64]{4,3,2,1,0:T(8,128)(2,1)} %ker_hbm.1, bf16[8,32,2,16,128]{4,3,2,1,0:T(8,128)(2,1)} %bitcast.2), custom_call_target="tpu_custom_call" | custom-call | tf_op jit(solution)/shard_map/conv_step/pallas_call | solution.py:392
  44.9 1.9 %write_out.1 = (bf16[8,32,2,16,128]{4,3,2,1,0:T(8,128)(2,1)}, bf16[64,2,16,128]{3,2,1,0:T(8,128)(2,1)}, f32[4,4,4,32,64]{4,3,2,1,0:T(8,128)}) custom-call(bf16[8,32,2,16,128]{4,3,2,1,0:T(8,128)(2,1)S(1)} %get-tuple-element.9.act, bf16[64,2,16,128]{3,2,1,0:T(8,128)(2,1)S(1)} %get-tuple-element.10.ig, bf16[2,256,256]{2,1,0:T(8,128)(2,1)S(1)} %get-tuple-element.11.fin), custom_call_target="tpu_custom_call" | custom-call | tf_op jit(solution)/shard_map/write_out/pallas_call | solution.py:436

commit v3 on v2

--- a/solution.py
+++ b/solution.py
@@ -34,7 +34,7 @@
 
 def step_kernel(
     scaling, vol_ref, ker_hbm, cot_ref, act_ref, igo, fin,
-    volb, ker_ref, face, turn, vt, cotb, cotf, actf, ua, ub, g_s, ak, bk, w_s,
+    volb, ker_ref, face, swap_rows, vt, cotb, cotn, actn, ua, ub, g_s, ak, bk, w_s,
     w_send, w_recv, w_bf, rs_in, part, z_in,
     igf, igb, igy, rx, ry, rc,
     l_sem, fs, fr, bs, br, ws, wr,
@@ -63,7 +63,13 @@
         (far_gx, gy), (sib_gx, gy), (gx, low_gy), (gx, high_gy),
         (far_gx, low_gy), (far_gx, high_gy), (sib_gx, low_gy), (sib_gx, high_gy),
     ]
-    peers = neighbours + [plane_peer(i)[1] for i in range(1, 16)] + [z_peer(i) for i in range(1, 4)]
+    order = sorted(range(1, 16), key=lambda i: -(min(i // 4, 4 - i // 4) + min(i % 4, 4 - i % 4)))
+
+    def twin(device):
+        return (device[0] + 1 - 2 * core, device[1])
+
+    plane = [plane_peer(i) for i in order]
+    peers = neighbours + [d for _, d in plane] + [twin(d) for _, d in plane] + [z_peer(i) for i in range(1, 4)]
 
     vol_copy = pltpu.make_async_copy(vol_ref, volb, l_sem.at[4])
     vol_copy.start()
@@ -82,27 +88,36 @@
     for peer in peers:
         pl.semaphore_signal(barrier, inc=1, device_id=peer, device_id_type=MESH)
 
-    def turn_in(get, slot):
-        turn[...] = get().astype(F32).reshape(64 * ROWS, 128)
-
-        def row(n, _):
-            vt[slot, :, lanes((n + 1) * 128, 128)] = turn[pl.ds(n, 64, stride=ROWS), :].astype(BF)
-            return 0
-
-        lax.fori_loop(0, ROWS, row, 0, unroll=True)
+    down_i = lax.broadcasted_iota(jnp.int32, (256, 256), 0)
+    along = lax.broadcasted_iota(jnp.int32, (256, 256), 1)
+    swapped = jnp.bitwise_or(jnp.left_shift(jnp.bitwise_and(along, 15), 4), jnp.right_shift(along, 4))
+    swap_rows[...] = jnp.where(down_i == swapped, 1.0, 0.0).astype(BF)
+
+    def swap16(value):
+        return jnp.dot(swap_rows[...], value, preferred_element_type=F32)
+
+    def turn_in(left, right, put_left, put_right):
+        both = swap16(jnp.concatenate([left.reshape(256, 128), right.reshape(256, 128)], axis=1)).astype(BF)
+        for n in range(ROWS):
+            put_left(n, both[16 * n:16 * n + 16, 0:128])
+            put_right(n, both[16 * n:16 * n + 16, 128:256])
+
+    def into(slot, group):
+        def put(n, value):
+            vt[slot, 16 * group:16 * group + 16, 128 * (n + 1):128 * (n + 2)] = value
+
+        return put
 
     vol_copy.wait()
-    turn_in(lambda: volb[:, 0], 1)
-    turn_in(lambda: volb[:, 1], 2)
+    for group in range(4):
+        rows16 = slice(16 * group, 16 * group + 16)
+        turn_in(volb[rows16, 0], volb[rows16, 1], into(1, group), into(2, group))
     pl.semaphore_wait(barrier, len(peers))
 
     sends = [
         remote(volb.at[:, core], face.at[0], fs.at[0], fr.at[0], neighbours[0]),
         remote(volb.at[:, other], face.at[1], fs.at[1], fr.at[1], neighbours[1]),
     ]
-    for copy in sends:
-        copy.start()
-
     first, last = pl.ds(128, 128), pl.ds(ROWS * 128, 128)
     low, high = pl.ds(0, 128), pl.ds((ROWS + 1) * 128, 128)
     own = pl.ds(1, 2)
@@ -114,7 +129,7 @@
         base = 4 + 2 * k
         ysends.append(remote(vt.at[1 + m, :, first], vt.at[slot, :, high], fs.at[base], fr.at[base], neighbours[base]))
         ysends.append(remote(vt.at[1 + m, :, last], vt.at[slot, :, low], fs.at[base + 1], fr.at[base + 1], neighbours[base + 1]))
-    for copy in ysends:
+    for copy in ysends[:2] + sends + ysends[2:]:
         copy.start()
     sends += ysends
 
@@ -130,6 +145,7 @@
             ak[p, q] = jnp.concatenate(pieces, axis=1) * half
     for a in range(4):
         bk[a] = ker_ref[a].reshape(512, 64).astype(F32).T.astype(BF) * half
+    w_s[...] = jnp.zeros((2, 2, 128, 256), F32)
     g_s[:, :, :, :, 0:256] = jnp.zeros((2, 2, 2, 128, 256), BF)
     g_s[:, :, :, :, 256 + WIDE:] = jnp.zeros((2, 2, 2, 128, 256), BF)
 
@@ -154,51 +170,80 @@
             axis=0,
         )
 
-    def block(k):
-        p, m = blocks[k]
+    def block(k, p, m):
         near, far = m + 1, m + 2 * p
-        cot_copies[k].wait()
-        cotf[...] = cotb[k].astype(F32).reshape(4 * 32 * ROWS, 128)
-
-        def product(t, dst):
+
+        def product(t):
             q, ci = t // 4, lax.rem(t, 4)
-            dst[...] = jnp.dot(
+            return jnp.dot(
                 ak[p, q], stacked(near, far, q, ci * 512, 512), preferred_element_type=F32
             )
 
-        def finish(t, src):
+        def finish(t, u):
             q, ci = t // 4, lax.rem(t, 4)
             for j in range(4):
                 n = ci * 4 + j
-                taps = [src[32 * c:32 * c + 32, 128 * j:128 * j + 128] for c in range(4)]
+                rows = pl.ds(pl.multiple_of(16 * n, 16), 16)
+                taps = [u[32 * c:32 * c + 32, 128 * j:128 * j + 128] for c in range(4)]
                 halves = (taps[1] + up(taps[3]), taps[2] + down(taps[0]))
                 grads = []
                 for s in range(2):
-                    rows = pl.ds((2 * q + s) * 32 * ROWS + n, 32, stride=ROWS)
                     t_h = jnp.tanh(halves[s])
                     w = 1.0 + t_h
                     act = halves[s] * w
-                    actf[rows, :] = act
-                    grads.append(cotf[rows, :] * (w + act * (1.0 - t_h)))
-                four = (up(grads[1]), grads[0], grads[1], down(grads[0]))
-                g_s[p, q, m, :, lanes((n + 2) * 128, 128)] = jnp.concatenate(
-                    [value.astype(BF) for value in four], axis=0
+                    slope = w + act * (1.0 - t_h)
+                    at = slice(128 * s, 128 * s + 128)
+                    act = act.astype(BF)
+                    for h in range(2):
+                        actn[k, q, h, rows, at] = act[16 * h:16 * h + 16]
+                    cot = jnp.concatenate([cotn[k, q, h, rows, at] for h in range(2)], axis=0)
+                    grads.append(cot * slope)
+                grads = [value.astype(BF) for value in grads]
+                four = (
+                    jnp.where(lane == 0, jnp.zeros((), BF), pltpu.roll(grads[1], 1, axis=1)),
+                    grads[0],
+                    grads[1],
+                    jnp.where(lane == 127, jnp.zeros((), BF), pltpu.roll(grads[0], 127, axis=1)),
                 )
-
-        product(0, ua)
+                g_s[p, q, m, :, lanes((n + 2) * 128, 128)] = jnp.concatenate(four, axis=0)
+
+        def grad(t):
+            q, ci = t // 4, lax.rem(t, 4)
+            w_s[p, q] += nt_dot(
+                g_s[p, q, m, :, lanes((4 * ci + 2) * 128, 512)], stacked(near, far, q, ci * 512, 512)
+            )
+
+        ua[...] = product(0)
+        ub[...] = product(1)
+        finish(0, ua)
 
         def pair(i, _):
-            product(2 * i + 1, ub)
-            finish(2 * i, ua)
-            product(jnp.minimum(2 * i + 2, 7), ua)
-            finish(2 * i + 1, ub)
+            t = 2 * i + 1
+            grad(t - 1)
+            ua[...] = product(t + 1)
+            finish(t, ub)
+            grad(t)
+            ub[...] = product(t + 2)
+            finish(t + 1, ua)
             return 0
 
-        lax.fori_loop(0, 4, pair, 0)
-        for q in range(2):
-            grad = nt_dot(g_s[p, q, m, :, 256:256 + WIDE], stacked(near, far, q, 0, WIDE))
-            w_s[p, q] = grad if k < 2 else w_s[p, q] + grad
-        act_ref[pl.ds(4 * p, 4), :, m] = actf[...].reshape(4, 32, ROWS, 128).astype(BF)
+        lax.fori_loop(0, 3, pair, 0)
+        grad(6)
+        finish(7, ub)
+        grad(7)
+
+    for copy in cot_copies:
+        copy.wait()
+
+    def turn_cot(i, _):
+        k, q, h = i // 4, lax.rem(i // 2, 2), lax.rem(i, 2)
+        pair = [
+            cotb[k, 2 * q + s, pl.ds(16 * h, 16)].reshape(256, 128) for s in range(2)
+        ]
+        cotn[k, q, h] = swap16(jnp.concatenate(pair, axis=1))
+        return 0
+
+    lax.fori_loop(0, 16, turn_cot, 0)
 
     ysends[0].wait_recv()
     ysends[1].wait_recv()
@@ -211,12 +256,20 @@
     def _():
         vt[own, :, high] = jnp.zeros((2, 64, 128), BF)
 
-    block(0)
-    block(1)
+    def early(k, _):
+        block(k, 1 - k, k)
+        return 0
+
+    lax.fori_loop(0, 2, early, 0)
 
     def halo(index, slot):
         sends[index].wait_recv()
-        turn_in(lambda: face[index], slot)
+        for group in (0, 2):
+            turn_in(
+                face[index, 16 * group:16 * group + 16],
+                face[index, 16 * group + 16:16 * group + 32],
+                into(slot, group), into(slot, group + 1),
+            )
         sends[4 + 2 * index].wait_recv()
         sends[5 + 2 * index].wait_recv()
 
@@ -229,7 +282,7 @@
             vt[slot, :, high] = jnp.zeros((64, 128), BF)
 
     halo(1, 3 - 3 * core)
-    block(2)
+    block(2, other, other)
     w_send[...] = w_s[other].reshape(256, 256).astype(BF)
     swap = remote(w_send, w_recv, ws.at[0], wr.at[0], neighbours[1])
     swap.start()
@@ -240,14 +293,13 @@
     def _():
         vt[3 * core] = jnp.zeros((64, HALO), BF)
 
-    block(3)
+    block(3, core, core)
 
     swap.wait_recv()
     w_s[core] = w_s[core] + w_recv[...].astype(F32).reshape(2, 128, 256)
     w_bf[...] = w_s[core].reshape(256, 256).astype(BF)
     scatter = []
-    for i in range(1, 16):
-        index, peer = plane_peer(i)
+    for i, (index, peer) in zip(order, plane):
         scatter.append(remote(w_bf.at[pl.ds(pl.multiple_of(16 * index, 16), 16)], rs_in.at[i], ws.at[1], wr.at[1], peer))
     for copy in scatter:
         copy.start()
@@ -305,15 +357,27 @@
     gather_z = [remote(part, z_in.at[z], ws.at[2], wr.at[2], z_peer(i)) for i in range(1, 4)]
     for copy in gather_z:
         copy.start()
+    for k, (p, m) in enumerate(blocks):
+
+        def turn_act(i, _, k=k, p=p, m=m):
+            q, h = i // 2, lax.rem(i, 2)
+            value = swap16(actn[k, q, h]).astype(BF)
+            for s in range(2):
+                act_ref[4 * p + 2 * q + s, pl.ds(16 * h, 16), m] = value[:, 128 * s:128 * s + 128].reshape(16, ROWS, 128)
+            return 0
+
+        lax.fori_loop(0, 4, turn_act, 0)
+
     three = z_in.at[pl.ds(0, 3)]
     remote(three, three, ws.at[2], wr.at[2], neighbours[1]).wait_recv()
     total = (z_in[0] + z_in[1]) + (z_in[2] + z_in[3])
     fin[core, pl.ds(pl.multiple_of(16 * mine, 16), 16)] = (total * (0.5 * scaling)).astype(BF)
     spread = []
-    for i in range(1, 16):
-        _, peer = plane_peer(i)
-        shard = fin.at[core, pl.ds(pl.multiple_of(16 * mine, 16), 16)]
+    shard = fin.at[core, pl.ds(pl.multiple_of(16 * mine, 16), 16)]
+    for _, peer in plane:
         spread.append(remote(shard, shard, ws.at[3], wr.at[3], peer))
+        spread.append(remote(shard, shard, ws.at[4], wr.at[4], twin(peer)))
+    spread.append(remote(shard, shard, ws.at[4], wr.at[4], neighbours[1]))
     for copy in spread:
         copy.start()
 
@@ -344,15 +408,21 @@
             add_face()
         add(4, 1, lambda index=index: rc[index, 0], m, jnp.logical_and(ok, jnp.logical_not(last_y)))
         add(5, 0, lambda index=index: rc[index, 1], m, jnp.logical_and(ok, jnp.logical_not(first_y)))
-        for n in range(ROWS):
-            turn[pl.ds(n, 64, stride=ROWS), :] = igf[m, :, pl.ds((n + 1) * 128, 128)]
-        igo[:, m] = turn[...].reshape(64, ROWS, 128).astype(BF)
-
+        for group in (0, 2):
+            halves = [
+                jnp.concatenate(
+                    [igf[m, 16 * g:16 * g + 16, 128 * (n + 1):128 * (n + 2)].astype(BF) for n in range(ROWS)], axis=0
+                )
+                for g in (group, group + 1)
+            ]
+            value = swap16(jnp.concatenate(halves, axis=1)).astype(BF)
+            for g in range(2):
+                at = 16 * (group + g)
+                igo[at:at + 16, m] = value[:, 128 * g:128 * g + 128].reshape(16, ROWS, 128)
     remote(w_bf.at[pl.ds(0, 240)], fin.at[core, pl.ds(0, 240)], ws.at[3], wr.at[3], neighbours[1]).wait_recv()
-    both = remote(fin.at[core], fin.at[core], ws.at[4], wr.at[4], neighbours[1])
-    both.start()
-    both.wait_recv()
-    for copy in sends + bsends + [swap, both]:
+    whole = remote(fin.at[core], fin.at[core], ws.at[4], wr.at[4], neighbours[1])
+    whole.wait_recv()
+    for copy in sends + bsends + [swap, whole]:
         copy.wait_send()
     remote(three, three, ws.at[2], wr.at[2], neighbours[1]).wait_send()
     remote(w_bf.at[pl.ds(0, 240)], fin.at[core, pl.ds(0, 240)], ws.at[1], wr.at[1], neighbours[1]).wait_send()
@@ -402,11 +472,11 @@
             pltpu.VMEM((64, 2, ROWS, 128), BF),
             pltpu.VMEM((4, 4, 4, 32, 64), BF),
             pltpu.VMEM((2, 64, ROWS, 128), BF),
-            pltpu.VMEM((64 * ROWS, 128), F32),
+            pltpu.VMEM((256, 256), BF),
             pltpu.VMEM((4, 64, HALO), BF),
             pltpu.VMEM((4, 4, 32, ROWS, 128), BF),
-            pltpu.VMEM((4 * 32 * ROWS, 128), F32),
-            pltpu.VMEM((4 * 32 * ROWS, 128), F32),
+            pltpu.VMEM((4, 2, 2, 256, 256), F32),
+            pltpu.VMEM((4, 2, 2, 256, 256), BF),
             pltpu.VMEM((128, 512), F32),
             pltpu.VMEM((128, 512), F32),
             pltpu.VMEM((2, 2, 2, 128, (ROWS + 4) * 128), BF),

time: 46.9 us -> 43 us (0.917)
  Pallas kernels: 46.1 us -> 42.2 us
    pallas_call x1, Pallas kernels: 44.3 us -> 40.3 us  [on_device(): pl.pallas_call(functools.partial(step_kernel, scaling), out_shape=(pltpu....]
where the time goes in v3:
time: 43 us; the launch traced here: 42.8 us
  Pallas kernels  42.2 us (98%)
  between operations  0.64 us (1%)
    pallas_call x1, Pallas kernels, on_device(): pl.pallas_call(functools.partial(step_kernel, scaling), out_shape=(pltpu....  40.3 us
    pallas_call x1, Pallas kernels, on_device(): pl.pallas_call(write_kernel, out_shape=(jax.ShapeDtypeStruct((8, 32, 2, R...  1.89 us

profile of v3, /device:TPU:1, one launch (start us, length us, event | category | flops | bytes accessed | tf_op | source)
XLA Modules:
  0.0 42.8 jit_solution(5088985122821329096)
XLA Ops:
  0.6 40.3 %conv_step.1 = (bf16[8,32,2,16,128]{4,3,2,1,0:T(8,128)(2,1)S(1)}, bf16[64,2,16,128]{3,2,1,0:T(8,128)(2,1)S(1)}, bf16[2,256,256]{2,1,0:T(8,128)(2,1)S(1)}) custom-call(bf16[64,2,16,128]{3,2,1,0:T(8,128)(2,1)} %vol_ref.1, bf16[4,4,4,32,64]{4,3,2,1,0:T(8,128)(2,1)} %ker_hbm.1, bf16[8,32,2,16,128]{4,3,2,1,0:T(8,128)(2,1)} %bitcast.2), custom_call_target="tpu_custom_call" | custom-call | tf_op jit(solution)/shard_map/conv_step/pallas_call | solution.py:462
  41.0 1.9 %write_out.1 = (bf16[8,32,2,16,128]{4,3,2,1,0:T(8,128)(2,1)}, bf16[64,2,16,128]{3,2,1,0:T(8,128)(2,1)}, f32[4,4,4,32,64]{4,3,2,1,0:T(8,128)}) custom-call(bf16[8,32,2,16,128]{4,3,2,1,0:T(8,128)(2,1)S(1)} %get-tuple-element.9.act, bf16[64,2,16,128]{3,2,1,0:T(8,128)(2,1)S(1)} %get-tuple-element.10.ig, bf16[2,256,256]{2,1,0:T(8,128)(2,1)S(1)} %get-tuple-element.11.fin), custom_call_target="tpu_custom_call" | custom-call | tf_op jit(solution)/shard_map/write_out/pallas_call | solution.py:506

commit v4 on v3

--- a/solution.py
+++ b/solution.py
@@ -15,6 +15,8 @@
 ROWS = 16
 WIDE = ROWS * 128
 HALO = (ROWS + 2) * 128
+EARLY = 2
+LEAD = 8
 
 
 def remote(src, dst, send, recv, device):
@@ -34,7 +36,7 @@
 
 def step_kernel(
     scaling, vol_ref, ker_hbm, cot_ref, act_ref, igo, fin,
-    volb, ker_ref, face, swap_rows, vt, cotb, cotn, actn, ua, ub, g_s, ak, bk, w_s,
+    volb, ker_ref, face, swap_rows, vt, cotb, cotn, actn, u_s, g_s, ak, bk, w_s,
     w_send, w_recv, w_bf, rs_in, part, z_in,
     igf, igb, igy, rx, ry, rc,
     l_sem, fs, fr, bs, br, ws, wr,
@@ -139,16 +141,16 @@
         for q in range(2):
             pieces = [
                 ker_ref[a, b].reshape(128, 64)
-                for a in (1 + p, 3 - 3 * p)
-                for b in (1 + q, 3 - 3 * q)
+                for a in (3 - p, 1 - p)
+                for b in (3 - q, 1 - q)
             ]
-            ak[p, q] = jnp.concatenate(pieces, axis=1) * half
+            ak[p, 128 * q:128 * q + 128] = jnp.concatenate(pieces, axis=1) * half
     for a in range(4):
         bk[a] = ker_ref[a].reshape(512, 64).astype(F32).T.astype(BF) * half
-    w_s[...] = jnp.zeros((2, 2, 128, 256), F32)
-    g_s[:, :, :, :, 0:256] = jnp.zeros((2, 2, 2, 128, 256), BF)
-    g_s[:, :, :, :, 256 + WIDE:] = jnp.zeros((2, 2, 2, 128, 256), BF)
-
+    w_s[...] = jnp.zeros((2, 256, 256), F32)
+    vt[:, :, HALO:] = jnp.zeros((4, 64, 384), BF)
+    for at, count in ((3, LEAD - 3), (LEAD + ROWS, 4)):
+        g_s[:, :, :, :, 128 * at:128 * (at + count)] = jnp.zeros((2, 2, 2, 128, 128 * count), BF)
 
     lane = lax.broadcasted_iota(jnp.int32, (32, 128), 1)
 
@@ -158,79 +160,83 @@
     def down(u):
         return jnp.where(lane == 127, 0.0, pltpu.roll(u, 127, axis=1))
 
-    def stacked(near, far, q, start, size):
-        shift = 2 * q
-        return jnp.concatenate(
-            [
-                vt[near, :, lanes(start + 128, size)],
-                vt[near, :, lanes(start + 128 * shift, size)],
-                vt[far, :, lanes(start + 128, size)],
-                vt[far, :, lanes(start + 128 * shift, size)],
-            ],
-            axis=0,
-        )
-
-    def block(k, p, m):
-        near, far = m + 1, m + 2 * p
-
-        def product(t):
-            q, ci = t // 4, lax.rem(t, 4)
-            return jnp.dot(
-                ak[p, q], stacked(near, far, q, ci * 512, 512), preferred_element_type=F32
+    def group(members, weights, low_x, w_at):
+        def tile(t):
+            start = 512 * jnp.maximum(t, 0)
+            return jnp.concatenate(
+                [
+                    vt[low_x + i, :, lanes(start + 128 * j, 512)]
+                    for i in range(2)
+                    for j in range(2)
+                ],
+                axis=0,
             )
 
-        def finish(t, u):
-            q, ci = t // 4, lax.rem(t, 4)
-            for j in range(4):
-                n = ci * 4 + j
-                rows = pl.ds(pl.multiple_of(16 * n, 16), 16)
-                taps = [u[32 * c:32 * c + 32, 128 * j:128 * j + 128] for c in range(4)]
-                halves = (taps[1] + up(taps[3]), taps[2] + down(taps[0]))
-                grads = []
-                for s in range(2):
-                    t_h = jnp.tanh(halves[s])
-                    w = 1.0 + t_h
-                    act = halves[s] * w
-                    slope = w + act * (1.0 - t_h)
-                    at = slice(128 * s, 128 * s + 128)
-                    act = act.astype(BF)
-                    for h in range(2):
-                        actn[k, q, h, rows, at] = act[16 * h:16 * h + 16]
-                    cot = jnp.concatenate([cotn[k, q, h, rows, at] for h in range(2)], axis=0)
-                    grads.append(cot * slope)
-                grads = [value.astype(BF) for value in grads]
-                four = (
-                    jnp.where(lane == 0, jnp.zeros((), BF), pltpu.roll(grads[1], 1, axis=1)),
-                    grads[0],
-                    grads[1],
-                    jnp.where(lane == 127, jnp.zeros((), BF), pltpu.roll(grads[0], 127, axis=1)),
-                )
-                g_s[p, q, m, :, lanes((n + 2) * 128, 128)] = jnp.concatenate(four, axis=0)
+        def product(t, slot):
+            u = jnp.dot(weights(), tile(t), preferred_element_type=F32)
+            u_s[slot, 0:len(members)] = u.reshape(len(members), 256, 512)
 
         def grad(t):
-            q, ci = t // 4, lax.rem(t, 4)
-            w_s[p, q] += nt_dot(
-                g_s[p, q, m, :, lanes((4 * ci + 2) * 128, 512)], stacked(near, far, q, ci * 512, 512)
-            )
-
-        ua[...] = product(0)
-        ub[...] = product(1)
-        finish(0, ua)
-
-        def pair(i, _):
-            t = 2 * i + 1
+            rows = [
+                g_s[p, q, m, :, lanes((4 * t - q + LEAD) * 128, 512)]
+                for _, p, m in members
+                for q in range(2)
+            ]
+            value = nt_dot(jnp.concatenate(rows, axis=0), tile(t))
+            w_s[w_at] += value.reshape(len(members), 256, 256)
+
+        def finish(t, slot, corners, sides):
+            for member, (k, p, m) in enumerate(members):
+                for j in range(corners):
+                    for q in sides:
+                        n = 4 * t + j - q
+                        if j == 0 and q == 1:
+                            outside = n < 0
+                            put = jnp.where(outside, ROWS, n)
+                            place = jnp.where(outside, LEAD + ROWS + 4, n + LEAD)
+                            take = jnp.maximum(n, 0)
+                        else:
+                            put, place, take = n, n + LEAD, n
+                        put = pl.ds(pl.multiple_of(16 * put, 16), 16)
+                        take = pl.ds(pl.multiple_of(16 * take, 16), 16)
+                        taps = [
+                            u_s[slot, member, 128 * q + 32 * c:128 * q + 32 * c + 32, 128 * j:128 * j + 128]
+                            for c in range(4)
+                        ]
+                        halves = (taps[1] + up(taps[3]), taps[2] + down(taps[0]))
+                        grads = []
+                        for s in range(2):
+                            t_h = jnp.tanh(halves[s])
+                            w = 1.0 + t_h
+                            act = halves[s] * w
+                            slope = w + act * (1.0 - t_h)
+                            at = slice(128 * s, 128 * s + 128)
+                            act = act.astype(BF)
+                            for h in range(2):
+                                actn[k, q, h, put, at] = act[16 * h:16 * h + 16]
+                            cot = jnp.concatenate([cotn[k, q, h, take, at] for h in range(2)], axis=0)
+                            grads.append((cot * slope).astype(BF))
+                        four = (
+                            jnp.where(lane == 0, jnp.zeros((), BF), pltpu.roll(grads[1], 1, axis=1)),
+                            grads[0],
+                            grads[1],
+                            jnp.where(lane == 127, jnp.zeros((), BF), pltpu.roll(grads[0], 127, axis=1)),
+                        )
+                        g_s[p, q, m, :, lanes(place * 128, 128)] = jnp.concatenate(four, axis=0)
+
+        product(0, 0)
+
+        def step(t, _):
+            now = lax.rem(t, 2)
             grad(t - 1)
-            ua[...] = product(t + 1)
-            finish(t, ub)
-            grad(t)
-            ub[...] = product(t + 2)
-            finish(t + 1, ua)
+            finish(t, now, 4, (0, 1))
+            product(t + 1, 1 - now)
             return 0
 
-        lax.fori_loop(0, 3, pair, 0)
-        grad(6)
-        finish(7, ub)
-        grad(7)
+        lax.fori_loop(0, ROWS // 4, step, 0)
+        grad(ROWS // 4 - 1)
+        finish(ROWS // 4, 0, 1, (1,))
+        grad(ROWS // 4)
 
     for copy in cot_copies:
         copy.wait()
@@ -256,11 +262,9 @@
     def _():
         vt[own, :, high] = jnp.zeros((2, 64, 128), BF)
 
-    def early(k, _):
-        block(k, 1 - k, k)
-        return 0
-
-    lax.fori_loop(0, 2, early, 0)
+    group(
+        [(1, 0, 1), (0, 1, 0)], lambda: ak[...].reshape(512, 256), 1, slice(0, 2)
+    )
 
     def halo(index, slot):
         sends[index].wait_recv()
@@ -282,8 +286,8 @@
             vt[slot, :, high] = jnp.zeros((64, 128), BF)
 
     halo(1, 3 - 3 * core)
-    block(2, other, other)
-    w_send[...] = w_s[other].reshape(256, 256).astype(BF)
+    group([(2, other, other)], lambda: ak[other], 2 * other, pl.ds(other, 1))
+    w_send[...] = w_s[other].astype(BF)
     swap = remote(w_send, w_recv, ws.at[0], wr.at[0], neighbours[1])
     swap.start()
 
@@ -291,13 +295,13 @@
 
     @pl.when(no_far)
     def _():
-        vt[3 * core] = jnp.zeros((64, HALO), BF)
-
-    block(3, core, core)
+        vt[3 * core] = jnp.zeros((64, HALO + 384), BF)
+
+    group([(3, core, core)], lambda: ak[core], 2 * core, pl.ds(core, 1))
 
     swap.wait_recv()
-    w_s[core] = w_s[core] + w_recv[...].astype(F32).reshape(2, 128, 256)
-    w_bf[...] = w_s[core].reshape(256, 256).astype(BF)
+    w_s[core] = w_s[core] + w_recv[...].astype(F32)
+    w_bf[...] = w_s[core].astype(BF)
     scatter = []
     for i, (index, peer) in zip(order, plane):
         scatter.append(remote(w_bf.at[pl.ds(pl.multiple_of(16 * index, 16), 16)], rs_in.at[i], ws.at[1], wr.at[1], peer))
@@ -308,7 +312,7 @@
         total = None
         for a, p, m in terms:
             parts = [
-                g_s[p, BACK[b][0], m, :, lanes((ci * 6 + 1 + BACK[b][1]) * 128, 768)]
+                g_s[p, BACK[b][0], m, :, lanes((ci * 6 + LEAD - 1 + BACK[b][1]) * 128, 768)]
                 for b in range(4)
             ]
             product = jnp.dot(bk[a], jnp.concatenate(parts, axis=0), preferred_element_type=F32)
@@ -322,11 +326,17 @@
 
     lax.fori_loop(0, 3, outer, 0)
     body = pl.ds(128, WIDE)
+    far_parts = []
+    for g in range(4):
+        rows16, at = pl.ds(16 * g, 16), 0 if g == 0 else 7 + g
+        far_parts.append(
+            remote(igb.at[core, rows16, body], rx.at[0, rows16], bs.at[at], br.at[at], neighbours[0])
+        )
     bsends = [
-        remote(igb.at[core, :, body], rx.at[0], bs.at[0], br.at[0], neighbours[0]),
+        far_parts[0],
         remote(igb.at[other, :, body], rx.at[1], bs.at[1], br.at[1], neighbours[1]),
     ]
-    for copy in bsends:
+    for copy in far_parts[:EARLY] + bsends[1:]:
         copy.start()
 
     def inner(ci, _):
@@ -348,20 +358,19 @@
 
     mine = 4 * x + y
     remote(w_bf.at[pl.ds(0, 240)].reshape(15, 16, 256), rs_in.at[pl.ds(1, 15)], ws.at[1], wr.at[1], neighbours[1]).wait_recv()
-    q = mine // 8
-    total = w_s[core, q, pl.ds(pl.multiple_of(16 * lax.rem(mine, 8), 16), 16)]
+    total = w_s[core, pl.ds(pl.multiple_of(16 * mine, 16), 16)]
     for i in range(1, 16):
         total = total + rs_in[i].astype(F32)
-    part[...] = total
-    z_in[z] = total
-    gather_z = [remote(part, z_in.at[z], ws.at[2], wr.at[2], z_peer(i)) for i in range(1, 4)]
-    for copy in gather_z:
+    part[...] = total.astype(BF)
+    z_in[z] = total.astype(BF)
+    gather_z = [remote(part, z_in.at[z], ws.at[2], wr.at[2], z_peer(i)) for i in (2, 1, 3)]
+    for copy in gather_z + far_parts[EARLY:3]:
         copy.start()
     for k, (p, m) in enumerate(blocks):
 
         def turn_act(i, _, k=k, p=p, m=m):
             q, h = i // 2, lax.rem(i, 2)
-            value = swap16(actn[k, q, h]).astype(BF)
+            value = swap16(actn[k, q, h, 0:256]).astype(BF)
             for s in range(2):
                 act_ref[4 * p + 2 * q + s, pl.ds(16 * h, 16), m] = value[:, 128 * s:128 * s + 128].reshape(16, ROWS, 128)
             return 0
@@ -370,7 +379,8 @@
 
     three = z_in.at[pl.ds(0, 3)]
     remote(three, three, ws.at[2], wr.at[2], neighbours[1]).wait_recv()
-    total = (z_in[0] + z_in[1]) + (z_in[2] + z_in[3])
+    wide = [z_in[i].astype(F32) for i in range(4)]
+    total = (wide[0] + wide[1]) + (wide[2] + wide[3])
     fin[core, pl.ds(pl.multiple_of(16 * mine, 16), 16)] = (total * (0.5 * scaling)).astype(BF)
     spread = []
     shard = fin.at[core, pl.ds(pl.multiple_of(16 * mine, 16), 16)]
@@ -378,7 +388,7 @@
         spread.append(remote(shard, shard, ws.at[3], wr.at[3], peer))
         spread.append(remote(shard, shard, ws.at[4], wr.at[4], twin(peer)))
     spread.append(remote(shard, shard, ws.at[4], wr.at[4], neighbours[1]))
-    for copy in spread:
+    for copy in spread + far_parts[3:]:
         copy.start()
 
     def add(index, k, src, m, keep):
@@ -395,7 +405,8 @@
         add(3, 0, lambda m=m: ry[1, m], m, jnp.logical_not(first_y))
     for index, m in ((1, other), (0, core)):
         ok = jnp.logical_not(no_far) if index == 0 else True
-        bsends[index].wait_recv()
+        for copy in far_parts if index == 0 else [bsends[1]]:
+            copy.wait_recv()
         bsends[4 + 2 * index].wait_recv()
         bsends[5 + 2 * index].wait_recv()
 
@@ -422,7 +433,7 @@
     remote(w_bf.at[pl.ds(0, 240)], fin.at[core, pl.ds(0, 240)], ws.at[3], wr.at[3], neighbours[1]).wait_recv()
     whole = remote(fin.at[core], fin.at[core], ws.at[4], wr.at[4], neighbours[1])
     whole.wait_recv()
-    for copy in sends + bsends + [swap, whole]:
+    for copy in sends + bsends + far_parts[1:] + [swap, whole]:
         copy.wait_send()
     remote(three, three, ws.at[2], wr.at[2], neighbours[1]).wait_send()
     remote(w_bf.at[pl.ds(0, 240)], fin.at[core, pl.ds(0, 240)], ws.at[1], wr.at[1], neighbours[1]).wait_send()
@@ -439,7 +450,7 @@
         copy.start()
     for p in range(2):
         for q in range(2):
-            taps = [(a, b) for a in (1 + p, 3 - 3 * p) for b in (1 + q, 3 - 3 * q)]
+            taps = [(a, b) for a in (3 - p, 1 - p) for b in (3 - q, 1 - q)]
             for i, (a, b) in enumerate(taps):
                 value = fin[p, 128 * q:128 * q + 128, 64 * i:64 * i + 64]
                 wgo[a, b] = value.astype(F32).reshape(4, 32, 64)
@@ -473,29 +484,28 @@
             pltpu.VMEM((4, 4, 4, 32, 64), BF),
             pltpu.VMEM((2, 64, ROWS, 128), BF),
             pltpu.VMEM((256, 256), BF),
-            pltpu.VMEM((4, 64, HALO), BF),
+            pltpu.VMEM((4, 64, HALO + 384), BF),
             pltpu.VMEM((4, 4, 32, ROWS, 128), BF),
             pltpu.VMEM((4, 2, 2, 256, 256), F32),
-            pltpu.VMEM((4, 2, 2, 256, 256), BF),
-            pltpu.VMEM((128, 512), F32),
-            pltpu.VMEM((128, 512), F32),
-            pltpu.VMEM((2, 2, 2, 128, (ROWS + 4) * 128), BF),
-            pltpu.VMEM((2, 2, 128, 256), BF),
+            pltpu.VMEM((4, 2, 2, 16 + 256, 256), BF),
+            pltpu.VMEM((2, 2, 256, 512), F32),
+            pltpu.VMEM((2, 2, 2, 128, (LEAD + ROWS + 5) * 128), BF),
+            pltpu.VMEM((2, 256, 256), BF),
             pltpu.VMEM((4, 64, 512), BF),
-            pltpu.VMEM((2, 2, 128, 256), F32),
+            pltpu.VMEM((2, 256, 256), F32),
             pltpu.VMEM((256, 256), BF),
             pltpu.VMEM((256, 256), BF),
             pltpu.VMEM((256, 256), BF),
             pltpu.VMEM((16, 16, 256), BF),
-            pltpu.VMEM((16, 256), F32),
-            pltpu.VMEM((4, 16, 256), F32),
+            pltpu.VMEM((16, 256), BF),
+            pltpu.VMEM((4, 16, 256), BF),
             pltpu.VMEM((2, 64, HALO), F32),
             pltpu.VMEM((2, 64, HALO), BF),
             pltpu.VMEM((2, 2, 64, 128), BF),
             pltpu.VMEM((2, 64, WIDE), BF),
             pltpu.VMEM((2, 2, 64, 128), BF),
             pltpu.VMEM((2, 2, 64, 128), BF),
-            dma((6,)), dma((8,)), dma((8,)), dma((8,)), dma((8,)), dma((5,)), dma((5,)),
+            dma((6,)), dma((8,)), dma((8,)), dma((11,)), dma((11,)), dma((5,)), dma((5,)),
         ],
         compiler_params=pltpu.CompilerParams(
             collective_id=0, has_side_effects=True, vmem_limit_bytes=40 * 1024 * 1024

time: 43 us -> 40.1 us (0.933)
  Pallas kernels: 42.2 us -> 39.4 us
    pallas_call x1, Pallas kernels: 40.3 us -> 37.5 us  [on_device(): pl.pallas_call(functools.partial(step_kernel, scaling), out_shape=(pltpu....]
where the time goes in v4:
time: 40.1 us; the launch traced here: 40 us
  Pallas kernels  39.4 us (98%)
  between operations  0.64 us (2%)
    pallas_call x1, Pallas kernels, on_device(): pl.pallas_call(functools.partial(step_kernel, scaling), out_shape=(pltpu....  37.5 us
    pallas_call x1, Pallas kernels, on_device(): pl.pallas_call(write_kernel, out_shape=(jax.ShapeDtypeStruct((8, 32, 2, R...  1.89 us

profile of v4, /device:TPU:1, one launch (start us, length us, event | category | flops | bytes accessed | tf_op | source)
XLA Modules:
  0.0 40.0 jit_solution(11543505345908538110)
XLA Ops:
  0.6 37.5 %conv_step.1 = (bf16[8,32,2,16,128]{4,3,2,1,0:T(8,128)(2,1)S(1)}, bf16[64,2,16,128]{3,2,1,0:T(8,128)(2,1)S(1)}, bf16[2,256,256]{2,1,0:T(8,128)(2,1)S(1)}) custom-call(bf16[64,2,16,128]{3,2,1,0:T(8,128)(2,1)} %vol_ref.1, bf16[4,4,4,32,64]{4,3,2,1,0:T(8,128)(2,1)} %ker_hbm.1, bf16[8,32,2,16,128]{4,3,2,1,0:T(8,128)(2,1)} %bitcast.2), custom_call_target="tpu_custom_call" | custom-call | tf_op jit(solution)/shard_map/conv_step/pallas_call | solution.py:473
  38.1 1.9 %write_out.1 = (bf16[8,32,2,16,128]{4,3,2,1,0:T(8,128)(2,1)}, bf16[64,2,16,128]{3,2,1,0:T(8,128)(2,1)}, f32[4,4,4,32,64]{4,3,2,1,0:T(8,128)}) custom-call(bf16[8,32,2,16,128]{4,3,2,1,0:T(8,128)(2,1)S(1)} %get-tuple-element.9.act, bf16[64,2,16,128]{3,2,1,0:T(8,128)(2,1)S(1)} %get-tuple-element.10.ig, bf16[2,256,256]{2,1,0:T(8,128)(2,1)S(1)} %get-tuple-element.11.fin), custom_call_target="tpu_custom_call" | custom-call | tf_op jit(solution)/shard_map/write_out/pallas_call | solution.py:516

commit v5 on v4

--- a/solution.py
+++ b/solution.py
@@ -148,8 +148,7 @@
     for a in range(4):
         bk[a] = ker_ref[a].reshape(512, 64).astype(F32).T.astype(BF) * half
     w_s[...] = jnp.zeros((2, 256, 256), F32)
-    vt[:, :, HALO:] = jnp.zeros((4, 64, 384), BF)
-    for at, count in ((3, LEAD - 3), (LEAD + ROWS, 4)):
+    for at, count in ((LEAD - 4, 5), (LEAD + ROWS, 2)):
         g_s[:, :, :, :, 128 * at:128 * (at + count)] = jnp.zeros((2, 2, 2, 128, 128 * count), BF)
 
     lane = lax.broadcasted_iota(jnp.int32, (32, 128), 1)
@@ -160,12 +159,11 @@
     def down(u):
         return jnp.where(lane == 127, 0.0, pltpu.roll(u, 127, axis=1))
 
-    def group(members, weights, low_x, w_at):
-        def tile(t):
-            start = 512 * jnp.maximum(t, 0)
+    def group(members, weights, low_x, w_at, between=None):
+        def tile(start, size):
             return jnp.concatenate(
                 [
-                    vt[low_x + i, :, lanes(start + 128 * j, 512)]
+                    vt[low_x + i, :, lanes(start + 128 * j, size)]
                     for i in range(2)
                     for j in range(2)
                 ],
@@ -173,28 +171,28 @@
             )
 
         def product(t, slot):
-            u = jnp.dot(weights(), tile(t), preferred_element_type=F32)
+            u = jnp.dot(weights(), tile(512 * t + 128, 512), preferred_element_type=F32)
             u_s[slot, 0:len(members)] = u.reshape(len(members), 256, 512)
 
-        def grad(t):
+        def grad(first, size):
             rows = [
-                g_s[p, q, m, :, lanes((4 * t - q + LEAD) * 128, 512)]
+                g_s[p, q, m, :, lanes((first - q + LEAD) * 128, size)]
                 for _, p, m in members
                 for q in range(2)
             ]
-            value = nt_dot(jnp.concatenate(rows, axis=0), tile(t))
+            value = nt_dot(jnp.concatenate(rows, axis=0), tile(128 * (jnp.maximum(first, 1) if size == 512 else first), size))
             w_s[w_at] += value.reshape(len(members), 256, 256)
 
-        def finish(t, slot, corners, sides):
+        def finish(first, slot, corners, sides):
             for member, (k, p, m) in enumerate(members):
                 for j in range(corners):
                     for q in sides:
-                        n = 4 * t + j - q
-                        if j == 0 and q == 1:
-                            outside = n < 0
-                            put = jnp.where(outside, ROWS, n)
-                            place = jnp.where(outside, LEAD + ROWS + 4, n + LEAD)
-                            take = jnp.maximum(n, 0)
+                        n = first + j - q
+                        if j == 3 and q == 0:
+                            outside = n == ROWS
+                            put = n
+                            place = jnp.where(outside, LEAD + ROWS + 2, n + LEAD)
+                            take = jnp.minimum(n, ROWS - 1)
                         else:
                             put, place, take = n, n + LEAD, n
                         put = pl.ds(pl.multiple_of(16 * put, 16), 16)
@@ -228,15 +226,22 @@
 
         def step(t, _):
             now = lax.rem(t, 2)
-            grad(t - 1)
-            finish(t, now, 4, (0, 1))
-            product(t + 1, 1 - now)
+            grad(4 * t - 3, 512)
+            finish(4 * t + 1, now, 4, (0, 1))
+            product(jnp.minimum(t + 1, 3), 1 - now)
             return 0
 
-        lax.fori_loop(0, ROWS // 4, step, 0)
-        grad(ROWS // 4 - 1)
-        finish(ROWS // 4, 0, 1, (1,))
-        grad(ROWS // 4)
+        if between is None:
+            lax.fori_loop(0, 4, step, 0)
+        else:
+            lax.fori_loop(0, 2, step, 0)
+            between()
+            lax.fori_loop(2, 4, step, 0)
+        u = jnp.dot(weights(), tile(0, 128), preferred_element_type=F32)
+        u_s[1, 0:len(members), :, 0:128] = u.reshape(len(members), 256, 128)
+        grad(13, 512)
+        finish(0, 1, 1, (0,))
+        grad(0, 128)
 
     for copy in cot_copies:
         copy.wait()
@@ -251,19 +256,20 @@
 
     lax.fori_loop(0, 16, turn_cot, 0)
 
-    ysends[0].wait_recv()
-    ysends[1].wait_recv()
-
-    @pl.when(first_y)
-    def _():
-        vt[own, :, low] = jnp.zeros((2, 64, 128), BF)
-
-    @pl.when(last_y)
-    def _():
-        vt[own, :, high] = jnp.zeros((2, 64, 128), BF)
+    def y_rows():
+        ysends[0].wait_recv()
+        ysends[1].wait_recv()
+
+        @pl.when(first_y)
+        def _():
+            vt[own, :, low] = jnp.zeros((2, 64, 128), BF)
+
+        @pl.when(last_y)
+        def _():
+            vt[own, :, high] = jnp.zeros((2, 64, 128), BF)
 
     group(
-        [(1, 0, 1), (0, 1, 0)], lambda: ak[...].reshape(512, 256), 1, slice(0, 2)
+        [(1, 0, 1), (0, 1, 0)], lambda: ak[...].reshape(512, 256), 1, slice(0, 2), y_rows
     )
 
     def halo(index, slot):
@@ -295,7 +301,7 @@
 
     @pl.when(no_far)
     def _():
-        vt[3 * core] = jnp.zeros((64, HALO + 384), BF)
+        vt[3 * core] = jnp.zeros((64, HALO), BF)
 
     group([(3, core, core)], lambda: ak[core], 2 * core, pl.ds(core, 1))
 
@@ -484,12 +490,12 @@
             pltpu.VMEM((4, 4, 4, 32, 64), BF),
             pltpu.VMEM((2, 64, ROWS, 128), BF),
             pltpu.VMEM((256, 256), BF),
-            pltpu.VMEM((4, 64, HALO + 384), BF),
+            pltpu.VMEM((4, 64, HALO), BF),
             pltpu.VMEM((4, 4, 32, ROWS, 128), BF),
             pltpu.VMEM((4, 2, 2, 256, 256), F32),
             pltpu.VMEM((4, 2, 2, 16 + 256, 256), BF),
             pltpu.VMEM((2, 2, 256, 512), F32),
-            pltpu.VMEM((2, 2, 2, 128, (LEAD + ROWS + 5) * 128), BF),
+            pltpu.VMEM((2, 2, 2, 128, (LEAD + ROWS + 3) * 128), BF),
             pltpu.VMEM((2, 256, 256), BF),
             pltpu.VMEM((4, 64, 512), BF),
             pltpu.VMEM((2, 256, 256), F32),

time: 40.1 us -> 39.3 us (0.980)
  Pallas kernels: 39.4 us -> 38.5 us
    pallas_call x1, Pallas kernels: 37.5 us -> 36.6 us  [on_device(): pl.pallas_call(functools.partial(step_kernel, scaling), out_shape=(pltpu....]
where the time goes in v5:
time: 39.3 us; the launch traced here: 39.1 us
  Pallas kernels  38.5 us (98%)
  between operations  0.64 us (2%)
    pallas_call x1, Pallas kernels, on_device(): pl.pallas_call(functools.partial(step_kernel, scaling), out_shape=(pltpu....  36.6 us
    pallas_call x1, Pallas kernels, on_device(): pl.pallas_call(write_kernel, out_shape=(jax.ShapeDtypeStruct((8, 32, 2, R...  1.89 us

profile of v5, /device:TPU:1, one launch (start us, length us, event | category | flops | bytes accessed | tf_op | source)
XLA Modules:
  0.0 39.1 jit_solution(9500609174955531346)
XLA Ops:
  0.6 36.6 %conv_step.1 = (bf16[8,32,2,16,128]{4,3,2,1,0:T(8,128)(2,1)S(1)}, bf16[64,2,16,128]{3,2,1,0:T(8,128)(2,1)S(1)}, bf16[2,256,256]{2,1,0:T(8,128)(2,1)S(1)}) custom-call(bf16[64,2,16,128]{3,2,1,0:T(8,128)(2,1)} %vol_ref.1, bf16[4,4,4,32,64]{4,3,2,1,0:T(8,128)(2,1)} %ker_hbm.1, bf16[8,32,2,16,128]{4,3,2,1,0:T(8,128)(2,1)} %bitcast.2), custom_call_target="tpu_custom_call" | custom-call | tf_op jit(solution)/shard_map/conv_step/pallas_call | solution.py:479
  37.2 1.9 %write_out.1 = (bf16[8,32,2,16,128]{4,3,2,1,0:T(8,128)(2,1)}, bf16[64,2,16,128]{3,2,1,0:T(8,128)(2,1)}, f32[4,4,4,32,64]{4,3,2,1,0:T(8,128)}) custom-call(bf16[8,32,2,16,128]{4,3,2,1,0:T(8,128)(2,1)S(1)} %get-tuple-element.9.act, bf16[64,2,16,128]{3,2,1,0:T(8,128)(2,1)S(1)} %get-tuple-element.10.ig, bf16[2,256,256]{2,1,0:T(8,128)(2,1)S(1)} %get-tuple-element.11.fin), custom_call_target="tpu_custom_call" | custom-call | tf_op jit(solution)/shard_map/write_out/pallas_call | solution.py:522

commit v6 on v5

--- a/solution.py
+++ b/solution.py
@@ -170,8 +170,8 @@
                 axis=0,
             )
 
-        def product(t, slot):
-            u = jnp.dot(weights(), tile(512 * t + 128, 512), preferred_element_type=F32)
+        def product(start, slot):
+            u = jnp.dot(weights(), tile(start, 512), preferred_element_type=F32)
             u_s[slot, 0:len(members)] = u.reshape(len(members), 256, 512)
 
         def grad(first, size):
@@ -222,13 +222,13 @@
                         )
                         g_s[p, q, m, :, lanes(place * 128, 128)] = jnp.concatenate(four, axis=0)
 
-        product(0, 0)
+        product(128, 0)
 
         def step(t, _):
             now = lax.rem(t, 2)
             grad(4 * t - 3, 512)
             finish(4 * t + 1, now, 4, (0, 1))
-            product(jnp.minimum(t + 1, 3), 1 - now)
+            product(jnp.where(t == 3, 0, 512 * t + 640), 1 - now)
             return 0
 
         if between is None:
@@ -237,10 +237,8 @@
             lax.fori_loop(0, 2, step, 0)
             between()
             lax.fori_loop(2, 4, step, 0)
-        u = jnp.dot(weights(), tile(0, 128), preferred_element_type=F32)
-        u_s[1, 0:len(members), :, 0:128] = u.reshape(len(members), 256, 128)
         grad(13, 512)
-        finish(0, 1, 1, (0,))
+        finish(0, 0, 1, (0,))
         grad(0, 128)
 
     for copy in cot_copies:

time: 39.3 us -> 39 us (level)
  Pallas kernels: 38.5 us -> 38.1 us
where the time goes in v6:
time: 39 us; the launch traced here: 38.8 us
  Pallas kernels  38.1 us (98%)
  between operations  0.64 us (2%)
    pallas_call x1, Pallas kernels, on_device(): pl.pallas_call(functools.partial(step_kernel, scaling), out_shape=(pltpu....  36.2 us
    pallas_call x1, Pallas kernels, on_device(): pl.pallas_call(write_kernel, out_shape=(jax.ShapeDtypeStruct((8, 32, 2, R...  1.89 us

profile of v6, /device:TPU:1, one launch (start us, length us, event | category | flops | bytes accessed | tf_op | source)
XLA Modules:
  0.0 38.8 jit_solution(7850572700520565189)
XLA Ops:
  0.6 36.2 %conv_step.1 = (bf16[8,32,2,16,128]{4,3,2,1,0:T(8,128)(2,1)S(1)}, bf16[64,2,16,128]{3,2,1,0:T(8,128)(2,1)S(1)}, bf16[2,256,256]{2,1,0:T(8,128)(2,1)S(1)}) custom-call(bf16[64,2,16,128]{3,2,1,0:T(8,128)(2,1)} %vol_ref.1, bf16[4,4,4,32,64]{4,3,2,1,0:T(8,128)(2,1)} %ker_hbm.1, bf16[8,32,2,16,128]{4,3,2,1,0:T(8,128)(2,1)} %bitcast.2), custom_call_target="tpu_custom_call" | custom-call | tf_op jit(solution)/shard_map/conv_step/pallas_call | solution.py:477
  36.9 1.9 %write_out.1 = (bf16[8,32,2,16,128]{4,3,2,1,0:T(8,128)(2,1)}, bf16[64,2,16,128]{3,2,1,0:T(8,128)(2,1)}, f32[4,4,4,32,64]{4,3,2,1,0:T(8,128)}) custom-call(bf16[8,32,2,16,128]{4,3,2,1,0:T(8,128)(2,1)S(1)} %get-tuple-element.9.act, bf16[64,2,16,128]{3,2,1,0:T(8,128)(2,1)S(1)} %get-tuple-element.10.ig, bf16[2,256,256]{2,1,0:T(8,128)(2,1)S(1)} %get-tuple-element.11.fin), custom_call_target="tpu_custom_call" | custom-call | tf_op jit(solution)/shard_map/write_out/pallas_call | solution.py:520
